TPU v7x, 32 devices: a whole 2x2x4 slice. The times are simulated.
32 devices in a mesh: ctx: 8 (over y, x, core), head: 4 (over z).
Axes of the slice: x: 2, y: 2, z: 4, core: 2. Of those that a mesh axis runs over, the one named last changes fastest.
Arguments:
- queries: bfloat16 [2048, 4096], P(('ctx', 'head')), may hold values from -0.59765625 to 0.59765625
- key_in: bfloat16 [2048, 4096], P(('ctx', 'head')), may hold values from -0.59765625 to 0.59765625
- values_in: bfloat16 [2048, 4096], P(('ctx', 'head')), may hold values from -6 to 6
- strength: bfloat16 [2048, 32], P(('ctx', 'head')), may hold values from 0 to 0.95, as said below
- log_decay: bfloat16 [2048, 4096], P(('ctx', 'head')), may hold values from -1.2 to 0, as said below
- d_out: bfloat16 [2048, 4096], P(('ctx', 'head')), may hold values from -6 to 6
Outputs:
- d_queries: bfloat16 [2048, 4096], P(('ctx', 'head'))
- d_keys: bfloat16 [2048, 4096], P(('ctx', 'head'))
- d_values: bfloat16 [2048, 4096], P(('ctx', 'head'))
- d_strength: bfloat16 [2048, 32], P(('ctx', 'head'))
- d_log_decay: bfloat16 [2048, 4096], P(('ctx', 'head'))
Inputs may be any that keep to these rules, and one draw needn't show every extreme that they name: `log_decay`: every log decay is negative. Every write strength is positive and below one.
All inputs are finite; a program needn't handle non-finite values.
Results may differ from a plain program's by a relative error of at most 0.00215.
Values may be sent and summed in bfloat16 or wider, within the bound.
A program may use at most 128 MiB of HBM per device.

v0:
```python
import jax
import jax.numpy as jnp
from jax import lax
from jax.sharding import PartitionSpec as P

SPAN = 64


exact_prec = lax.Precision.HIGHEST
epsilon = 1e-06


def passed_along(value, axis, steps):
    count = lax.axis_size(axis)
    leading, last = (max(0, -steps), min(count, count - steps))
    return lax.ppermute(value, axis, [(source, source + steps) for source in range(leading, last)])


def prepare(queries, keys_used, values_used, strength, log_decay):
    span_len = queries.shape[1]
    head_width = queries.shape[3]
    q_unit = (
        queries
        * lax.rsqrt(jnp.sum(queries * queries, axis=3, keepdims=True) + epsilon)
        * head_width ** (-0.5)
    )
    k_unit = keys_used * lax.rsqrt(jnp.sum(keys_used * keys_used, axis=3, keepdims=True) + epsilon)
    gamma = jnp.cumsum(log_decay, axis=1)
    middle = gamma[:, span_len // 2 - 1 : span_len // 2]
    q_rise = q_unit * jnp.exp(gamma - middle)
    k_rise = k_unit * jnp.exp(gamma - middle)
    k_fall = k_unit * jnp.exp(middle - gamma)
    strict_mask = jnp.tril(jnp.ones((span_len, span_len), jnp.float32), -1)
    causal_mask = jnp.tril(jnp.ones((span_len, span_len), jnp.float32))
    key_inner = jnp.einsum("ntha,nsha->nhts", k_rise, k_fall, precision=exact_prec) * strict_mask
    scores = jnp.einsum("ntha,nsha->nhts", q_rise, k_fall, precision=exact_prec) * causal_mask
    strength_t = jnp.transpose(strength, (0, 2, 1))
    system = jnp.eye(span_len, dtype=jnp.float32) + strength_t[..., None] * key_inner
    k_head = k_unit * jnp.exp(gamma)
    right_side = jnp.concatenate([values_used, k_head], axis=3) * strength[..., None]
    right_side = jnp.transpose(right_side, (0, 2, 1, 3))
    solved = lax.linalg.triangular_solve(
        system, right_side, left_side=True, lower=True, unit_diagonal=True
    )
    w_value = solved[..., :head_width]
    w_key = solved[..., head_width:]
    gamma_end = gamma[:, -1:]
    key_tail = k_unit * jnp.exp(gamma_end - gamma)
    fade_last = jnp.exp(gamma_end[:, 0])
    q_head = q_unit * jnp.exp(gamma)
    return (q_head, scores, w_value, w_key, key_tail, fade_last)


def march(w_value, w_key, key_tail, fade_last, state):

    def advance(state_now, piece_data):
        value_part, key_part, tail_part, fade_part = piece_data
        updates = value_part - jnp.einsum("hta,hab->htb", key_part, state_now, precision=exact_prec)
        following = fade_part[:, :, None] * state_now + jnp.einsum(
            "tha,htb->hab", tail_part, updates, precision=exact_prec
        )
        return (following, (state_now, updates))

    final_state, (start_states, all_updates) = lax.scan(
        advance, state, (w_value, w_key, key_tail, fade_last)
    )
    return (final_state, start_states, all_updates)


def sweep(prepared, state):
    q_head, scores, w_value, w_key, key_tail, fade_last = prepared
    final_state, start_states, all_updates = march(w_value, w_key, key_tail, fade_last, state)
    output = jnp.einsum("ntha,nhab->nthb", q_head, start_states, precision=exact_prec)
    output = output + jnp.einsum("nhts,nhsb->nthb", scores, all_updates, precision=exact_prec)
    return (output, final_state)


def compose(matrix, state):
    return jnp.einsum("hab,hbc->hac", matrix, state, precision=exact_prec)


def per_device(queries, key_in, values_in, strength, log_decay, d_out):
    heads_all = strength.shape[1]
    local_heads = heads_all // lax.axis_size("head")
    head_width = queries.shape[1] // heads_all
    moved = (
        lax.all_to_all(queries, "head", split_axis=1, concat_axis=0, tiled=True),
        lax.all_to_all(key_in, "head", split_axis=1, concat_axis=0, tiled=True),
        lax.all_to_all(values_in, "head", split_axis=1, concat_axis=0, tiled=True),
        lax.all_to_all(log_decay, "head", split_axis=1, concat_axis=0, tiled=True),
        lax.all_to_all(d_out, "head", split_axis=1, concat_axis=0, tiled=True),
        lax.all_to_all(strength, "head", split_axis=1, concat_axis=0, tiled=True),
    )
    query_local, key_local, value_local, decay_local, grad_local, strength_local = moved
    row_count = query_local.shape[0]
    blocks = row_count // SPAN

    def shaped(array):
        return array.astype(jnp.float32).reshape(blocks, SPAN, local_heads, head_width)

    strength_blocks = strength_local.astype(jnp.float32).reshape(blocks, SPAN, local_heads)
    prepared, pull_prep = jax.vjp(
        prepare,
        shaped(query_local),
        shaped(key_local),
        shaped(value_local),
        strength_blocks,
        shaped(decay_local),
    )
    q_head, scores, w_value, w_key, key_tail, fade_last = prepared
    unit_matrix = jnp.broadcast_to(
        jnp.eye(head_width, dtype=jnp.float32), (local_heads, head_width, head_width)
    )
    zero_state = jnp.zeros((local_heads, head_width, head_width), jnp.float32)
    wide_start = jnp.concatenate([zero_state, unit_matrix], axis=2)
    wide_value = jnp.concatenate([w_value, jnp.zeros_like(w_value)], axis=3)
    ends = march(wide_value, w_key, key_tail, fade_last, wide_start)[0]
    offset = ends[..., :head_width]
    transfer = ends[..., head_width:]
    transfer_t = jnp.transpose(transfer, (0, 2, 1))
    cot_out = shaped(grad_local)

    def outputs_of(state):
        return sweep(prepared, state)[0]

    _, pull_state = jax.vjp(outputs_of, zero_state)
    inject = pull_state(cot_out)[0]
    n_context = lax.axis_size("ctx")

    def forward_turn(turn_index, relay_pair):
        leaving, arriving = relay_pair
        arriving = passed_along(leaving, "ctx", 1)
        return (compose(transfer, arriving) + offset, arriving)

    state_in = lax.fori_loop(0, n_context, forward_turn, (offset, zero_state))[1]

    def backward_turn(turn_index, relay_pair):
        leaving, arriving = relay_pair
        arriving = passed_along(leaving, "ctx", -1)
        return (compose(transfer_t, arriving) + inject, arriving)

    grad_in = lax.fori_loop(0, n_context, backward_turn, (inject, zero_state))[1]

    def sweep_prepared(prepared_in):
        return sweep(prepared_in, state_in)

    _, pull_sweep = jax.vjp(sweep_prepared, prepared)
    d_prepared = pull_sweep((cot_out, grad_in))[0]
    d_query, d_key, d_value, d_strength, d_decay = pull_prep(d_prepared)

    def flatten(array):
        return array.reshape(row_count, local_heads * head_width).astype(jnp.bfloat16)

    strength_grad = d_strength.reshape(row_count, local_heads).astype(jnp.bfloat16)
    returned = (
        lax.all_to_all(flatten(d_query), "head", split_axis=0, concat_axis=1, tiled=True),
        lax.all_to_all(flatten(d_key), "head", split_axis=0, concat_axis=1, tiled=True),
        lax.all_to_all(flatten(d_value), "head", split_axis=0, concat_axis=1, tiled=True),
        lax.all_to_all(flatten(d_decay), "head", split_axis=0, concat_axis=1, tiled=True),
        lax.all_to_all(strength_grad, "head", split_axis=0, concat_axis=1, tiled=True),
    )
    return (returned[0], returned[1], returned[2], returned[4], returned[3])


def solution(mesh):
    in_specs = (
        P(("ctx", "head"), None),
        P(("ctx", "head"), None),
        P(("ctx", "head"), None),
        P(("ctx", "head"), None),
        P(("ctx", "head"), None),
        P(("ctx", "head"), None),
    )
    out_specs = (
        P(("ctx", "head"), None),
        P(("ctx", "head"), None),
        P(("ctx", "head"), None),
        P(("ctx", "head"), None),
        P(("ctx", "head"), None),
    )
    return jax.shard_map(
        per_device, mesh=mesh, in_specs=in_specs, out_specs=out_specs, check_vma=False
    )
```

profile of v0, /device:TPU:4, one launch (start us, length us, event | category | flops | bytes accessed | tf_op | source)
XLA Modules:
  0.0 746.2 jit_solution(3267437615622263255)
XLA Ops:
  2.0 4.9 all-to-all-start.2
  12.5 5.0 all-to-all-start
  18.8 12.7 %all-to-all-done = bf16[64,4,1024]{2,0,1:T(8,128)(2,1)S(1)} async-done(((bf16[64,4,1024]{2,0,1:T(8,128)(2,1)}), bf16[64,4,1024]{2,0,1:T(8,128)(2,1)S(1)}, u32[]{:S(2)}, u32[]{:S(2)}) %all-to-all-start) | async-done | bytes 524320 | tf_op jit(solution)/shard_map/all_to_all | solution.py:90
  36.1 13.6 %all-to-all-done.1 = bf16[64,4,1024]{2,0,1:T(8,128)(2,1)} async-done(((bf16[64,4,1024]{2,0,1:T(8,128)(2,1)}), bf16[64,4,1024]{2,0,1:T(8,128)(2,1)}, u32[]{:S(2)}, u32[]{:S(2)}) %all-to-all-start.1) | async-done | bytes 524320 | tf_op jit(solution)/shard_map/all_to_all | solution.py:88
  62.2 158.7 %custom-call.7 = f32[4,8,1,64,64]{3,4,2,1,0:T(8,128)} custom-call(f32[4,8,1,64,64]{4,3,2,1,0:T(8,128)} %add_bitcast_fusion.1), custom_call_target="InvertDiagBlocksLowerTriangular" | custom-call | tf_op jit(solution)/shard_map/jvp()/triangular_solve | solution.py:42
  224.7 5.1 all-to-all-start.5
  231.1 5.2 broadcast_select_fusion
  238.4 16.3 %while.97 = (s32[]{:T(128)}, f32[8,128,256]{2,1,0:T(8,128)S(1)}, f32[4,8,128]{2,1,0:T(8,128)S(1)}, f32[4,64,8,128]{3,1,2,0:T(8,128)}, f32[4,8,64,256]{3,2,1,0:T(8,128)}, /*index=5*/f32[4,8,64,128]{3,2,1,0:T(8,128)}, s32[]{:T(128)}) while((s32[]{:T(128)}, f32[8,128,256]{2,1,0:T(8,128)S(1)}, f32[4,8,128]{2,1,0:T(8,128)S(1)}, ...), condition=%wide.region_3.4_spmd, body=%wide.region_2.0_spmd.sunk | while | flops 403308544 | bytes 5256785 | solution.py:64
  257.6 5.3 all-to-all-start.4
  266.5 4.5 convolution_multiply_fusion
  271.1 4.7 all-to-all-done.4
  275.9 4.9 fusion.61
  282.4 16.3 %while.103 = (s32[]{:T(128)}, f32[8,128,128]{2,1,0:T(8,128)S(1)}, f32[4,8,128,128]{3,2,1,0:T(8,128)}, f32[4,8,128,1]{2,1,3,0:T(8,128)S(1)}, f32[4,8,64,128]{3,2,...) while((s32[]{:T(128)}, f32[8,128,128]{2,1,0:T(8,128)S(1)}, ...), condition=%wide.region_13.14_spmd.clone, body=%wide.region_12.13_spmd.clone.sunk | while | flops 202113024 | bytes 3423358 | solution.py:64
  305.2 115.5 %while.98 = (s32[]{:T(128)}, f32[8,128,128]{2,1,0:T(8,128)}, f32[8,128,128]{2,1,0:T(8,128)}, f32[8,128,128]{2,1,0:T(8,128)}, f32[8,128,128]{2,1,0:T(8,128)}, /*index=5*/s32[]{:T(128)}) while((s32[]{:T(128)}, f32[8,128,128]{2,1,0:T(8,128)}, f32[8,128,128]{2,1,0:T(8,128)}, f32[8,128,128]{2,1,0:T(8,128)}, f32[8,128,128]{2,1,0:T(8,128)}, ...), condition=%wide.region_5.6_spmd, body=%wide.region_4.5_spmd.sunk | while | flops 201457664 | bytes 6291593 | solution.py:135
  307.1 9.7 %collective-permute-done = f32[8,128,128]{2,1,0:T(8,128)S(1)} collective-permute-done((f32[8,128,128]{2,1,0:T(8,128)}, f32[8,128,128]{2,1,0:T(8,128)S(1)}, u32[]{:S(2)}, u32[]{:S(2)}) %collective-permute-start) | collective-permute-done | bytes 524320 | tf_op jit(solution)/shard_map/while/body/eval_jaxpr/ppermute | solution.py:16
  321.5 9.7 %collective-permute-done = f32[8,128,128]{2,1,0:T(8,128)S(1)} collective-permute-done((f32[8,128,128]{2,1,0:T(8,128)}, f32[8,128,128]{2,1,0:T(8,128)S(1)}, u32[]{:S(2)}, u32[]{:S(2)}) %collective-permute-start) | collective-permute-done | bytes 524320 | tf_op jit(solution)/shard_map/while/body/eval_jaxpr/ppermute | solution.py:16
  336.0 9.7 %collective-permute-done = f32[8,128,128]{2,1,0:T(8,128)S(1)} collective-permute-done((f32[8,128,128]{2,1,0:T(8,128)}, f32[8,128,128]{2,1,0:T(8,128)S(1)}, u32[]{:S(2)}, u32[]{:S(2)}) %collective-permute-start) | collective-permute-done | bytes 524320 | tf_op jit(solution)/shard_map/while/body/eval_jaxpr/ppermute | solution.py:16
  350.4 9.7 %collective-permute-done = f32[8,128,128]{2,1,0:T(8,128)S(1)} collective-permute-done((f32[8,128,128]{2,1,0:T(8,128)}, f32[8,128,128]{2,1,0:T(8,128)S(1)}, u32[]{:S(2)}, u32[]{:S(2)}) %collective-permute-start) | collective-permute-done | bytes 524320 | tf_op jit(solution)/shard_map/while/body/eval_jaxpr/ppermute | solution.py:16
  364.8 9.7 %collective-permute-done = f32[8,128,128]{2,1,0:T(8,128)S(1)} collective-permute-done((f32[8,128,128]{2,1,0:T(8,128)}, f32[8,128,128]{2,1,0:T(8,128)S(1)}, u32[]{:S(2)}, u32[]{:S(2)}) %collective-permute-start) | collective-permute-done | bytes 524320 | tf_op jit(solution)/shard_map/while/body/eval_jaxpr/ppermute | solution.py:16
  379.3 9.7 %collective-permute-done = f32[8,128,128]{2,1,0:T(8,128)S(1)} collective-permute-done((f32[8,128,128]{2,1,0:T(8,128)}, f32[8,128,128]{2,1,0:T(8,128)S(1)}, u32[]{:S(2)}, u32[]{:S(2)}) %collective-permute-start) | collective-permute-done | bytes 524320 | tf_op jit(solution)/shard_map/while/body/eval_jaxpr/ppermute | solution.py:16
  393.7 9.7 %collective-permute-done = f32[8,128,128]{2,1,0:T(8,128)S(1)} collective-permute-done((f32[8,128,128]{2,1,0:T(8,128)}, f32[8,128,128]{2,1,0:T(8,128)S(1)}, u32[]{:S(2)}, u32[]{:S(2)}) %collective-permute-start) | collective-permute-done | bytes 524320 | tf_op jit(solution)/shard_map/while/body/eval_jaxpr/ppermute | solution.py:16
  408.1 9.7 %collective-permute-done = f32[8,128,128]{2,1,0:T(8,128)S(1)} collective-permute-done((f32[8,128,128]{2,1,0:T(8,128)}, f32[8,128,128]{2,1,0:T(8,128)S(1)}, u32[]{:S(2)}, u32[]{:S(2)}) %collective-permute-start) | collective-permute-done | bytes 524320 | tf_op jit(solution)/shard_map/while/body/eval_jaxpr/ppermute | solution.py:16
  421.8 29.4 %while.99 = (s32[]{:T(128)}, f32[8,128,128]{2,1,0:T(8,128)}, f32[4,8,128,128]{3,2,1,0:T(8,128)}, f32[4,8,64,128]{3,2,1,0:T(8,128)}, f32[4,8,128,1]{2,1,3,0:T(8,1...) while((s32[]{:T(128)}, f32[8,128,128]{2,1,0:T(8,128)}, ...), condition=%wide.region_7.8_spmd, body=%wide.region_6.7_spmd.sunk | while | flops 201654272 | bytes 8411301 | solution.py:64
  452.0 111.5 %while.101 = (s32[]{:T(128)}, f32[8,128,128]{2,1,0:T(8,128)}, f32[8,128,128]{2,1,0:T(8,128)}, f32[8,128,128]{2,1,0:T(8,128)}, f32[8,128,128]{2,1,0:T(8,128)S(1)}, /*index=5*/s32[]{:T(128)}) while((s32[]{:T(128)}, f32[8,128,128]{2,1,0:T(8,128)}, f32[8,128,128]{2,1,0:T(8,128)}, f32[8,128,128]{2,1,0:T(8,128)}, f32[8,128,128]{2,1,0:T(8,128)S(1)}, ...), condition=%wide.region_15.16_spmd, body=%wide.region_14.15_spmd.sunk | while | flops 201457664 | bytes 6291593 | solution.py:142
  453.9 7.0 collective-permute-done.1
  463.6 4.6 collective-permute-start.1
  468.2 7.0 collective-permute-done.1
  477.8 4.6 collective-permute-start.1
  482.4 7.0 collective-permute-done.1
  492.1 4.6 collective-permute-start.1
  496.7 7.0 collective-permute-done.1
  506.4 4.6 collective-permute-start.1
  511.0 7.0 collective-permute-done.1
  520.6 4.6 collective-permute-start.1
  525.3 7.0 collective-permute-done.1
  534.9 4.6 collective-permute-start.1
  539.5 7.0 collective-permute-done.1
  549.2 4.6 collective-permute-start.1
  553.8 7.0 collective-permute-done.1
  566.8 56.1 %while.102 = (s32[]{:T(128)}, f32[8,128,128]{2,1,0:T(8,128)S(1)}, f32[4,8,64,128]{3,2,1,0:T(8,128)}, f32[4,8,64,128]{3,2,1,0:T(8,128)}, f32[4,64,8,128]{3,1,2,0:...) while((s32[]{:T(128)}, f32[8,128,128]{2,1,0:T(8,128)S(1)}, ...), condition=%wide.region_18.19_spmd, body=%wide.region_16.18_spmd.sunk | while | flops 403504128 | bytes 6844581 | solution.py:64
  622.9 6.0 fusion.40
  658.6 15.8 %reduce_window_sum.26 = bf16[4,64,1024]{2,1,0:T(8,128)(2,1)} reduce-window(f32[4,64,1024]{2,1,0:T(8,128)} %bitcast.430, f32[]{:T(128)} %constant.177.clone.1), window={size=1x64x1 pad=0_0x0_63x0_0}, to_apply=%region_26.27 | reduce-window | flops 16515072 | bytes 1572868 | tf_op jit(solution)/shard_map/transpose(jvp(jit(cumsum)))/reduce_window_sum | solution.py:28
  674.4 5.1 all-to-all-start.10
  680.4 11.4 %all-to-all-done.10 = bf16[4,64,1024]{2,1,0:T(8,128)(2,1)S(1)} async-done(((bf16[4,64,1024]{2,1,0:T(8,128)(2,1)}), bf16[4,64,1024]{2,1,0:T(8,128)(2,1)S(1)}, u32[]{:S(2)}, u32[]{:S(2)}) %all-to-all-start.10) | async-done | bytes 524320 | tf_op jit(solution)/shard_map/all_to_all | solution.py:159
  691.8 5.3 all-to-all-start.7
  698.5 13.9 %all-to-all-done.7 = bf16[4,64,1024]{2,1,0:T(8,128)(2,1)S(1)} async-done(((bf16[4,64,1024]{2,1,0:T(8,128)(2,1)}), bf16[4,64,1024]{2,1,0:T(8,128)(2,1)S(1)}, u32[]{:S(2)}, u32[]{:S(2)}) %all-to-all-start.7) | async-done | bytes 524320 | tf_op jit(solution)/shard_map/all_to_all | solution.py:157
  718.0 13.2 %all-to-all-done.6 = bf16[4,64,1024]{2,1,0:T(8,128)(2,1)S(1)} async-done(((bf16[4,64,1024]{2,1,0:T(8,128)(2,1)}), bf16[4,64,1024]{2,1,0:T(8,128)(2,1)S(1)}, u32[]{:S(2)}, u32[]{:S(2)}) %all-to-all-start.6) | async-done | bytes 524320 | tf_op jit(solution)/shard_map/all_to_all | solution.py:156
  737.9 7.1 all-to-all-done.8
  (308 shorter events, 266.5 us)
Async XLA Ops:
  0.6 10.1 %copy-start.32 = (bf16[64,4096]{1,0:T(8,128)(2,1)S(1)}, bf16[64,4096]{1,0:T(8,128)(2,1)}, u32[]{:S(2)}) copy-start(bf16[64,4096]{1,0:T(8,128)(2,1)} %param.22) | copy-start | bytes 1572868
  0.7 10.9 %copy-start.33 = (bf16[64,4096]{1,0:T(8,128)(2,1)S(1)}, bf16[64,4096]{1,0:T(8,128)(2,1)}, u32[]{:S(2)}) copy-start(bf16[64,4096]{1,0:T(8,128)(2,1)} %param.20) | copy-start | bytes 1572868
  2.0 10.5 %all-to-all-start.2 = ((bf16[4,2,256]{2,1,0:T(2,128)(2,1)}), bf16[4,2,256]{2,1,0:T(2,128)(2,1)S(1)}, u32[]{:S(2)}, u32[]{:S(2)}) async-start(bf16[4,2,256]{2,1,0:T(2,128)(2,1)} %reshape.209), calls=%async_computation.2 | async-start | bytes 8192 | tf_op jit(solution)/shard_map/all_to_all | solution.py:92
  8.8 8.8 %copy-start.34 = (bf16[64,4096]{1,0:T(8,128)(2,1)S(1)}, bf16[64,4096]{1,0:T(8,128)(2,1)}, u32[]{:S(2)}) copy-start(bf16[64,4096]{1,0:T(8,128)(2,1)} %param.25) | copy-start | bytes 1572868
  12.5 19.0 %all-to-all-start = ((bf16[64,4,1024]{2,0,1:T(8,128)(2,1)}), bf16[64,4,1024]{2,0,1:T(8,128)(2,1)S(1)}, u32[]{:S(2)}, u32[]{:S(2)}) async-start(bf16[64,4,1024]{2,0,1:T(8,128)(2,1)} %bitcast.347), calls=%async_computation | async-start | bytes 1048576 | tf_op jit(solution)/shard_map/all_to_all | solution.py:90
  31.4 18.3 %all-to-all-start.1 = ((bf16[64,4,1024]{2,0,1:T(8,128)(2,1)}), bf16[64,4,1024]{2,0,1:T(8,128)(2,1)}, u32[]{:S(2)}, u32[]{:S(2)}) async-start(bf16[64,4,1024]{2,0,1:T(8,128)(2,1)} %bitcast.346), calls=%async_computation.1 | async-start | bytes 1048576 | tf_op jit(solution)/shard_map/all_to_all | solution.py:88
  49.7 174.2 %all-to-all-start.3 = ((bf16[64,4,1024]{2,0,1:T(8,128)(2,1)}), bf16[64,4,1024]{2,0,1:T(8,128)(2,1)S(1)}, u32[]{:S(2)}, u32[]{:S(2)}) async-start(bf16[64,4,1024]{2,0,1:T(8,128)(2,1)} %bitcast.437), calls=%async_computation.3 | async-start | bytes 1048576 | tf_op jit(solution)/shard_map/all_to_all | solution.py:89
  223.9 7.1 copy-start.35
  224.7 32.1 %all-to-all-start.5 = ((bf16[64,4,1024]{2,0,1:T(8,128)(2,1)}), bf16[64,4,1024]{2,0,1:T(8,128)(2,1)S(1)}, u32[]{:S(2)}, u32[]{:S(2)}) async-start(bf16[64,4,1024]{2,0,1:T(8,128)(2,1)} %bitcast.436), calls=%async_computation.5 | async-start | bytes 1048576 | tf_op jit(solution)/shard_map/all_to_all | solution.py:87
  231.0 5.4 copy-start.25
  257.6 18.3 %all-to-all-start.4 = ((bf16[64,4,1024]{2,0,1:T(8,128)(2,1)}), bf16[64,4,1024]{2,0,1:T(8,128)(2,1)S(1)}, u32[]{:S(2)}, u32[]{:S(2)}) async-start(bf16[64,4,1024]{2,0,1:T(8,128)(2,1)} %bitcast.435), calls=%async_computation.4 | async-start | bytes 1048576 | tf_op jit(solution)/shard_map/all_to_all | solution.py:91
  275.9 4.9 copy-start.14
  275.9 4.9 copy-start.29
  305.2 11.6 %collective-permute-start = (f32[8,128,128]{2,1,0:T(8,128)}, f32[8,128,128]{2,1,0:T(8,128)S(1)}, u32[]{:S(2)}, u32[]{:S(2)}) collective-permute-start(f32[8,128,128]{2,1,0:T(8,128)} %get-tuple-element.1199), channel_id=1, source_target_pairs={{0,4},{4,8},{8,12},{12,16},{16,20},{20,24},{24,28},{1,5},{5,9},{9,... | collective-permute-start | bytes 1572872 | tf_op jit(solution)/shard_map/while/body/eval_jaxpr/ppermute | solution.py:16
  319.6 11.6 %collective-permute-start = (f32[8,128,128]{2,1,0:T(8,128)}, f32[8,128,128]{2,1,0:T(8,128)S(1)}, u32[]{:S(2)}, u32[]{:S(2)}) collective-permute-start(f32[8,128,128]{2,1,0:T(8,128)} %get-tuple-element.1199), channel_id=1, source_target_pairs={{0,4},{4,8},{8,12},{12,16},{16,20},{20,24},{24,28},{1,5},{5,9},{9,... | collective-permute-start | bytes 1572872 | tf_op jit(solution)/shard_map/while/body/eval_jaxpr/ppermute | solution.py:16
  334.1 11.6 %collective-permute-start = (f32[8,128,128]{2,1,0:T(8,128)}, f32[8,128,128]{2,1,0:T(8,128)S(1)}, u32[]{:S(2)}, u32[]{:S(2)}) collective-permute-start(f32[8,128,128]{2,1,0:T(8,128)} %get-tuple-element.1199), channel_id=1, source_target_pairs={{0,4},{4,8},{8,12},{12,16},{16,20},{20,24},{24,28},{1,5},{5,9},{9,... | collective-permute-start | bytes 1572872 | tf_op jit(solution)/shard_map/while/body/eval_jaxpr/ppermute | solution.py:16
  348.5 11.6 %collective-permute-start = (f32[8,128,128]{2,1,0:T(8,128)}, f32[8,128,128]{2,1,0:T(8,128)S(1)}, u32[]{:S(2)}, u32[]{:S(2)}) collective-permute-start(f32[8,128,128]{2,1,0:T(8,128)} %get-tuple-element.1199), channel_id=1, source_target_pairs={{0,4},{4,8},{8,12},{12,16},{16,20},{20,24},{24,28},{1,5},{5,9},{9,... | collective-permute-start | bytes 1572872 | tf_op jit(solution)/shard_map/while/body/eval_jaxpr/ppermute | solution.py:16
  362.9 11.6 %collective-permute-start = (f32[8,128,128]{2,1,0:T(8,128)}, f32[8,128,128]{2,1,0:T(8,128)S(1)}, u32[]{:S(2)}, u32[]{:S(2)}) collective-permute-start(f32[8,128,128]{2,1,0:T(8,128)} %get-tuple-element.1199), channel_id=1, source_target_pairs={{0,4},{4,8},{8,12},{12,16},{16,20},{20,24},{24,28},{1,5},{5,9},{9,... | collective-permute-start | bytes 1572872 | tf_op jit(solution)/shard_map/while/body/eval_jaxpr/ppermute | solution.py:16
  377.4 11.6 %collective-permute-start = (f32[8,128,128]{2,1,0:T(8,128)}, f32[8,128,128]{2,1,0:T(8,128)S(1)}, u32[]{:S(2)}, u32[]{:S(2)}) collective-permute-start(f32[8,128,128]{2,1,0:T(8,128)} %get-tuple-element.1199), channel_id=1, source_target_pairs={{0,4},{4,8},{8,12},{12,16},{16,20},{20,24},{24,28},{1,5},{5,9},{9,... | collective-permute-start | bytes 1572872 | tf_op jit(solution)/shard_map/while/body/eval_jaxpr/ppermute | solution.py:16
  391.8 11.6 %collective-permute-start = (f32[8,128,128]{2,1,0:T(8,128)}, f32[8,128,128]{2,1,0:T(8,128)S(1)}, u32[]{:S(2)}, u32[]{:S(2)}) collective-permute-start(f32[8,128,128]{2,1,0:T(8,128)} %get-tuple-element.1199), channel_id=1, source_target_pairs={{0,4},{4,8},{8,12},{12,16},{16,20},{20,24},{24,28},{1,5},{5,9},{9,... | collective-permute-start | bytes 1572872 | tf_op jit(solution)/shard_map/while/body/eval_jaxpr/ppermute | solution.py:16
  406.2 11.6 %collective-permute-start = (f32[8,128,128]{2,1,0:T(8,128)}, f32[8,128,128]{2,1,0:T(8,128)S(1)}, u32[]{:S(2)}, u32[]{:S(2)}) collective-permute-start(f32[8,128,128]{2,1,0:T(8,128)} %get-tuple-element.1199), channel_id=1, source_target_pairs={{0,4},{4,8},{8,12},{12,16},{16,20},{20,24},{24,28},{1,5},{5,9},{9,... | collective-permute-start | bytes 1572872 | tf_op jit(solution)/shard_map/while/body/eval_jaxpr/ppermute | solution.py:16
  421.8 4.4 copy-start.5
  429.1 4.5 copy-start.5
  436.5 4.4 copy-start.5
  443.8 4.4 copy-start.5
  452.0 8.9 %collective-permute-start.1 = (f32[8,128,128]{2,1,0:T(8,128)}, f32[8,128,128]{2,1,0:T(8,128)S(1)}, u32[]{:S(2)}, u32[]{:S(2)}) collective-permute-start(f32[8,128,128]{2,1,0:T(8,128)} %get-tuple-element.1289), channel_id=1, source_target_pairs={{4,0},{8,4},{12,8},{16,12},{20,16},{24,20},{28,24},{5,1},{9,5},{13... | collective-permute-start | bytes 1572872 | tf_op jit(solution)/shard_map/while/body/eval_jaxpr/ppermute | solution.py:16
  463.6 11.6 %collective-permute-start.1 = (f32[8,128,128]{2,1,0:T(8,128)}, f32[8,128,128]{2,1,0:T(8,128)S(1)}, u32[]{:S(2)}, u32[]{:S(2)}) collective-permute-start(f32[8,128,128]{2,1,0:T(8,128)} %get-tuple-element.1289), channel_id=1, source_target_pairs={{4,0},{8,4},{12,8},{16,12},{20,16},{24,20},{28,24},{5,1},{9,5},{13... | collective-permute-start | bytes 1572872 | tf_op jit(solution)/shard_map/while/body/eval_jaxpr/ppermute | solution.py:16
  477.8 11.6 %collective-permute-start.1 = (f32[8,128,128]{2,1,0:T(8,128)}, f32[8,128,128]{2,1,0:T(8,128)S(1)}, u32[]{:S(2)}, u32[]{:S(2)}) collective-permute-start(f32[8,128,128]{2,1,0:T(8,128)} %get-tuple-element.1289), channel_id=1, source_target_pairs={{4,0},{8,4},{12,8},{16,12},{20,16},{24,20},{28,24},{5,1},{9,5},{13... | collective-permute-start | bytes 1572872 | tf_op jit(solution)/shard_map/while/body/eval_jaxpr/ppermute | solution.py:16
  492.1 11.6 %collective-permute-start.1 = (f32[8,128,128]{2,1,0:T(8,128)}, f32[8,128,128]{2,1,0:T(8,128)S(1)}, u32[]{:S(2)}, u32[]{:S(2)}) collective-permute-start(f32[8,128,128]{2,1,0:T(8,128)} %get-tuple-element.1289), channel_id=1, source_target_pairs={{4,0},{8,4},{12,8},{16,12},{20,16},{24,20},{28,24},{5,1},{9,5},{13... | collective-permute-start | bytes 1572872 | tf_op jit(solution)/shard_map/while/body/eval_jaxpr/ppermute | solution.py:16
  506.4 11.6 %collective-permute-start.1 = (f32[8,128,128]{2,1,0:T(8,128)}, f32[8,128,128]{2,1,0:T(8,128)S(1)}, u32[]{:S(2)}, u32[]{:S(2)}) collective-permute-start(f32[8,128,128]{2,1,0:T(8,128)} %get-tuple-element.1289), channel_id=1, source_target_pairs={{4,0},{8,4},{12,8},{16,12},{20,16},{24,20},{28,24},{5,1},{9,5},{13... | collective-permute-start | bytes 1572872 | tf_op jit(solution)/shard_map/while/body/eval_jaxpr/ppermute | solution.py:16
  520.6 11.6 %collective-permute-start.1 = (f32[8,128,128]{2,1,0:T(8,128)}, f32[8,128,128]{2,1,0:T(8,128)S(1)}, u32[]{:S(2)}, u32[]{:S(2)}) collective-permute-start(f32[8,128,128]{2,1,0:T(8,128)} %get-tuple-element.1289), channel_id=1, source_target_pairs={{4,0},{8,4},{12,8},{16,12},{20,16},{24,20},{28,24},{5,1},{9,5},{13... | collective-permute-start | bytes 1572872 | tf_op jit(solution)/shard_map/while/body/eval_jaxpr/ppermute | solution.py:16
  534.9 11.6 %collective-permute-start.1 = (f32[8,128,128]{2,1,0:T(8,128)}, f32[8,128,128]{2,1,0:T(8,128)S(1)}, u32[]{:S(2)}, u32[]{:S(2)}) collective-permute-start(f32[8,128,128]{2,1,0:T(8,128)} %get-tuple-element.1289), channel_id=1, source_target_pairs={{4,0},{8,4},{12,8},{16,12},{20,16},{24,20},{28,24},{5,1},{9,5},{13... | collective-permute-start | bytes 1572872 | tf_op jit(solution)/shard_map/while/body/eval_jaxpr/ppermute | solution.py:16
  549.2 11.6 %collective-permute-start.1 = (f32[8,128,128]{2,1,0:T(8,128)}, f32[8,128,128]{2,1,0:T(8,128)S(1)}, u32[]{:S(2)}, u32[]{:S(2)}) collective-permute-start(f32[8,128,128]{2,1,0:T(8,128)} %get-tuple-element.1289), channel_id=1, source_target_pairs={{4,0},{8,4},{12,8},{16,12},{20,16},{24,20},{28,24},{5,1},{9,5},{13... | collective-permute-start | bytes 1572872 | tf_op jit(solution)/shard_map/while/body/eval_jaxpr/ppermute | solution.py:16
  622.9 6.0 copy-start.13
  622.9 6.0 copy-start.18
  622.9 6.0 copy-start.19
  641.5 32.9 %all-to-all-start.9 = ((bf16[4,2,256]{2,1,0:T(2,128)(2,1)}), bf16[4,2,256]{2,1,0:T(2,128)(2,1)S(1)}, u32[]{:S(2)}, u32[]{:S(2)}) async-start(bf16[4,2,256]{2,1,0:T(2,128)(2,1)} %reshape.211), calls=%async_computation.9 | async-start | bytes 8192 | tf_op jit(solution)/shard_map/all_to_all | solution.py:160
  645.0 4.2 copy-start.11
  645.0 6.5 copy-start.20
  645.0 6.5 copy-start.21
  645.0 6.5 copy-start.22
  658.6 38.5 %copy-start.10 = (f32[4,8,8,8,128]{4,3,2,1,0:T(8,128)S(1)}, f32[4,8,8,8,128]{4,3,2,1,0:T(8,128)}, u32[]{:S(2)}) copy-start(f32[4,8,8,8,128]{4,3,2,1,0:T(8,128)} %get-tuple-element.858) | copy-start | bytes 3145732
  658.6 38.5 %copy-start.28 = (f32[4,64,8,128]{3,1,2,0:T(8,128)S(1)}, f32[4,64,8,128]{3,1,2,0:T(8,128)}, u32[]{:S(2)}) copy-start(f32[4,64,8,128]{3,1,2,0:T(8,128)} %get-tuple-element.840) | copy-start | bytes 3145732
  674.4 17.4 %all-to-all-start.10 = ((bf16[4,64,1024]{2,1,0:T(8,128)(2,1)}), bf16[4,64,1024]{2,1,0:T(8,128)(2,1)S(1)}, u32[]{:S(2)}, u32[]{:S(2)}) async-start(bf16[4,64,1024]{2,1,0:T(8,128)(2,1)} %reduce_window_sum.26), calls=%async_computation.10 | async-start | bytes 1048576 | tf_op jit(solution)/shard_map/all_to_all | solution.py:159
  691.8 20.6 %all-to-all-start.7 = ((bf16[4,64,1024]{2,1,0:T(8,128)(2,1)}), bf16[4,64,1024]{2,1,0:T(8,128)(2,1)S(1)}, u32[]{:S(2)}, u32[]{:S(2)}) async-start(bf16[4,64,1024]{2,1,0:T(8,128)(2,1)} %bitcast.441), calls=%async_computation.7 | async-start | bytes 1048576 | tf_op jit(solution)/shard_map/all_to_all | solution.py:157
  712.4 18.8 %all-to-all-start.6 = ((bf16[4,64,1024]{2,1,0:T(8,128)(2,1)}), bf16[4,64,1024]{2,1,0:T(8,128)(2,1)S(1)}, u32[]{:S(2)}, u32[]{:S(2)}) async-start(bf16[4,64,1024]{2,1,0:T(8,128)(2,1)} %copy_bitcast_fusion.4), calls=%async_computation.6 | async-start | bytes 1048576 | tf_op jit(solution)/shard_map/all_to_all | solution.py:156
  731.2 13.7 %all-to-all-start.8 = ((bf16[4,64,1024]{2,1,0:T(8,128)(2,1)}), bf16[4,64,1024]{2,1,0:T(8,128)(2,1)S(1)}, u32[]{:S(2)}, u32[]{:S(2)}) async-start(bf16[4,64,1024]{2,1,0:T(8,128)(2,1)} %copy_bitcast_fusion.2), calls=%async_computation.8 | async-start | bytes 1048576 | tf_op jit(solution)/shard_map/all_to_all | solution.py:158
  735.4 10.4 %copy-start.1 = (bf16[64,32]{0,1:T(8,128)(2,1)S(1)}, bf16[64,32]{0,1:T(8,128)(2,1)}, u32[]{:S(2)}) copy-start(bf16[64,32]{0,1:T(8,128)(2,1)} %param.23) | copy-start | bytes 12292
  (35 other events, 75.4 us)
where the time goes:
time: 758 us; the launch traced here: 746 us
  waiting for transfers between devices  210 us (28%)
  other arithmetic  194 us (26%)
  matrix products  184 us (24%)
  starting transfers between devices  98 us (13%)
  local copies, waits for them, and re-layouts  48.1 us (6%)
  loops' own time  10.5 us (1%)
    another operation x5, other arithmetic, prepare(): lax.linalg.triangular_solve(system, right_side, left_side=True, lower=Tru...  160 us
    ppermute x16, waiting for transfers between devices, passed_along(): lax.ppermute(value, axis, [(source, source + steps) for source in range(l...  133 us
    ppermute x16, starting transfers between devices, passed_along(): lax.ppermute(value, axis, [(source, source + steps) for source in range(l...  49.4 us
    dot_general x20, matrix products, advance(): jnp.einsum('hta,hab->htb', key_part, state_now, precision=exact_prec)  47.8 us
    dot_general x20, matrix products, advance(): jnp.einsum('tha,htb->hab', tail_part, updates, precision=exact_prec)  44.1 us
    dot_general x16, matrix products, compose(): return jnp.einsum('hab,hbc->hac', matrix, state, precision=exact_prec)  44 us
    another operation x2, other arithmetic, prepare(): gamma = jnp.cumsum(log_decay, axis=1)  15.9 us
  transfers between devices with their start and end apart: 27, of which 24 were waited for; matrix products, arithmetic and copies ran while one was open for 33% of the time, Pallas kernels for 0%

commit v1 on v0

v1 whole, which is shorter than its diff:
```python
import functools

import jax
import jax.numpy as jnp
from jax import lax
from jax.experimental import pallas as pl
from jax.experimental.pallas import tpu as pltpu
from jax.sharding import PartitionSpec as P

SPAN = 64
BASE = 8
EPS = 1e-06
F32 = jnp.float32
BF16 = jnp.bfloat16
exact_prec = lax.Precision.HIGHEST

NN = (((1,), (0,)), ((), ()))
NT = (((1,), (1,)), ((), ()))


def split(x):
    high = x.astype(BF16)
    return high, (x - high.astype(F32)).astype(BF16)


def mul(a, b, dims=NN):
    return lax.dot_general(a, b, dims, preferred_element_type=F32)


def dot3(a, b, dims=NN):
    if not isinstance(a, tuple):
        return mul(a, b[0], dims) + mul(a, b[1], dims)
    if not isinstance(b, tuple):
        return mul(a[0], b, dims) + mul(a[1], b, dims)
    return mul(a[0], b[0], dims) + (mul(a[0], b[1], dims) + mul(a[1], b[0], dims))


def rows_of(pair, start, size):
    if not isinstance(pair, tuple):
        return pair[start : start + size]
    return tuple(part[start : start + size] for part in pair)


def both(a, b, axis):
    return tuple(jnp.concatenate([x, y], axis=axis) for x, y in zip(a, b))


def grids(size):
    return (
        lax.broadcasted_iota(jnp.int32, (size, size), 0),
        lax.broadcasted_iota(jnp.int32, (size, size), 1),
    )


def per_span(row_values, span, like):
    rows, width = like.shape
    return jnp.broadcast_to(row_values, (rows // span, span, width)).reshape(rows, width)


def gates(g, span):
    rows, width = g.shape
    row, col = grids(rows)
    sum_mask = jnp.where((row // span == col // span) & (col <= row), 1.0, 0.0).astype(BF16)
    gamma = mul(sum_mask, g)
    spans = gamma.reshape(rows // span, span, width)
    middle = spans[:, span // 2 - 1 : span // 2]
    end = spans[:, span - 1 : span]
    centred = gamma - per_span(middle, span, gamma)
    rise = jnp.exp(centred)
    fall = jnp.exp(-centred)
    head = rise * per_span(jnp.exp(middle), span, gamma)
    tail = fall * per_span(jnp.exp(end - middle), span, gamma)
    fade = jnp.exp(end).reshape(rows // span, width)
    return rise, fall, head, tail, fade


def column_of(table, index):
    lane = lax.broadcasted_iota(jnp.int32, table.shape, 1)
    return jnp.sum(jnp.where(lane == index, table, 0.0), axis=1, keepdims=True)


def norm_of(x):
    return lax.rsqrt(jnp.sum(x * x, axis=1, keepdims=True) + EPS)


def inverse(system, row, col):
    same = row // BASE == col // BASE
    near = jnp.where(same, system, 0.0)
    near_s = split(near)
    square = dot3(near_s, near_s)
    square_s = split(square)
    found = jnp.where(row == col, 1.0, 0.0) - near
    fourth = dot3(square_s, square_s)
    found = found + dot3(split(found), square_s)
    found = found + dot3(split(found), split(fourth))
    block = BASE
    while block < SPAN:
        wide = row // (2 * block) == col // (2 * block)
        off = jnp.where(wide & (row // block != col // block), system, 0.0)
        found_s = split(found)
        found = found - dot3(found_s, split(dot3(split(off), found_s)))
        block *= 2
    return found


def local_kernel(span, q_ref, k_ref, v_ref, g_ref, o_ref, b_ref, ev_ref, ek_ref, inv_ref, a_ref, sc_ref,
                 tr_ref, bs_ref, gs_ref, end_ref, trans_ref, inject_ref):
    head_index = pl.program_id(0)
    rows, width = q_ref.shape
    spans = rows // span
    q = q_ref[...].astype(F32)
    k = k_ref[...].astype(F32)
    v = v_ref[...]
    o = o_ref[...]
    beta = column_of(b_ref[...], head_index)
    rise, fall, head, tail, fade = gates(g_ref[...], span)
    q_unit = q * norm_of(q) * width ** (-0.5)
    k_unit = k * norm_of(k)
    row, col = grids(rows)
    inside = row // span == col // span
    k_fall_s = split(k_unit * fall)
    inner = jnp.where(inside & (col < row), dot3(split(k_unit * rise), k_fall_s, NT), 0.0)
    scores = jnp.where(inside & (col <= row), dot3(split(q_unit * rise), k_fall_s, NT), 0.0)
    a_ref[0] = inner
    sc_ref[0] = scores
    beta_row = jnp.sum(jnp.where(row == col, beta, 0.0), axis=0, keepdims=True)
    found = inverse(inner * beta_row, row, col)
    inv_ref[0] = found
    found_s = split(found)
    e_value = dot3(found_s, v)
    e_key = dot3(found_s, split(k_unit * head))
    ev_ref[0] = e_value
    ek_ref[0] = e_key
    w_key_s = split(e_key * beta)
    w_value_s = split(e_value * beta)
    reach = q_unit * head - dot3(split(scores), w_key_s)
    k_tail = k_unit * tail
    small_row, small_col = grids(width)
    diagonal = small_row == small_col
    moves, adds, backs = [], [], []
    for index in range(spans):
        at = index * span
        tail_t = split(k_tail[at : at + span].T)
        move = jnp.where(diagonal, fade[index : index + 1], 0.0) - dot3(tail_t, rows_of(w_key_s, at, span))
        add = dot3(tail_t, rows_of(w_value_s, at, span))
        back = dot3(split(reach[at : at + span].T), o[at : at + span])
        tr_ref[0, index] = move
        bs_ref[0, index] = add
        gs_ref[0, index] = back
        moves.append(move)
        adds.append(add)
        backs.append(back)
    trans, ends = moves[0], adds[0]
    grad = backs[spans - 1]
    for index in range(1, spans):
        move_s = split(moves[index])
        trans = dot3(move_s, split(trans))
        ends = dot3(move_s, split(ends)) + adds[index]
        mirror = spans - 1 - index
        grad = dot3(split(moves[mirror].T), split(grad)) + backs[mirror]
    trans_ref[0] = trans
    end_ref[0] = ends
    inject_ref[0] = grad


def grad_kernel(span, q_ref, k_ref, v_ref, g_ref, o_ref, b_ref, ev_ref, ek_ref, inv_ref, a_ref, sc_ref,
                tr_ref, bs_ref, gs_ref, state_ref, dstate_ref, dq_ref, dk_ref, dv_ref, dg_ref, db_ref):
    head_index = pl.program_id(0)
    rows, width = q_ref.shape
    spans = rows // span
    q = q_ref[...].astype(F32)
    k = k_ref[...].astype(F32)
    o = o_ref[...]
    beta = column_of(b_ref[...], head_index)
    rise, fall, head, tail, fade = gates(g_ref[...], span)
    q_norm = norm_of(q)
    k_norm = norm_of(k)
    q_unit = q * q_norm * width ** (-0.5)
    k_unit = k * k_norm
    row, col = grids(rows)
    inside = row // span == col // span
    states = [state_ref[0]]
    grads = [dstate_ref[0]]
    for index in range(spans - 1):
        states.append(dot3(split(tr_ref[0, index]), split(states[-1])) + bs_ref[0, index])
        mirror = spans - 1 - index
        grads.insert(0, dot3(split(tr_ref[0, mirror].T), split(grads[0])) + gs_ref[0, mirror])
    states_s = [split(x) for x in states]
    grads_s = [split(x) for x in grads]

    def each(fn):
        return jnp.concatenate([fn(index, index * span) for index in range(spans)], axis=0)

    ek_s = split(ek_ref[0])
    k_tail = k_unit * tail
    k_tail_s = split(k_tail)
    error = ev_ref[0] - each(lambda i, at: dot3(rows_of(ek_s, at, span), states_s[i]))
    update_s = split(error * beta)
    d_update = dot3(split(sc_ref[0].T), o) + each(lambda i, at: dot3(rows_of(k_tail_s, at, span), grads_s[i]))
    d_value = dot3(split(inv_ref[0].T), split(d_update * beta))
    d_value_s = split(d_value)
    dv_ref[...] = d_value.astype(BF16)
    residue = d_update - dot3(split(a_ref[0].T), d_value_s)
    d_beta = jnp.sum(error * residue, axis=1, keepdims=True)
    lane = lax.broadcasted_iota(jnp.int32, b_ref.shape, 1)
    db_ref[...] = jnp.where(lane == head_index, d_beta, db_ref[...])
    dq_head = each(lambda i, at: dot3(o[at : at + span], states_s[i], NT))
    dk_head = -each(lambda i, at: dot3(rows_of(d_value_s, at, span), states_s[i], NT))
    dk_tail = each(lambda i, at: dot3(rows_of(update_s, at, span), grads_s[i], NT))
    d_scores = jnp.where(inside & (col <= row), dot3(o, update_s, NT), 0.0)
    d_inner = jnp.where(inside & (col < row), -dot3(d_value_s, update_s, NT), 0.0)
    k_fall_s = split(k_unit * fall)
    dq_rise = dot3(split(d_scores), k_fall_s)
    dk_rise = dot3(split(d_inner), k_fall_s)
    dk_fall = dot3(split(d_scores.T), split(q_unit * rise)) + dot3(split(d_inner.T), split(k_unit * rise))
    dq_unit = dq_rise * rise + dq_head * head
    up = dk_rise * rise + dk_head * head
    tail_part = dk_tail * tail
    down = dk_fall * fall + tail_part
    d_gamma = q_unit * dq_unit + k_unit * (up - down)
    tail_sum = jnp.sum((k_unit * tail_part).reshape(spans, span, width), axis=1, keepdims=True)
    small_row, small_col = grids(width)
    diagonal = small_row == small_col
    last = []
    for index in range(spans):
        d_fade = jnp.sum(states[index] * grads[index], axis=1, keepdims=True)
        d_fade = jnp.sum(jnp.where(diagonal, d_fade, 0.0), axis=0, keepdims=True)
        last.append(d_fade * fade[index : index + 1])
    last = jnp.concatenate([x.reshape(1, 1, width) for x in last], axis=0)
    sum_mask = jnp.where(inside & (col >= row), 1.0, 0.0).astype(BF16)
    d_decay = dot3(sum_mask, split(d_gamma)) + per_span(tail_sum + last, span, d_gamma)
    dg_ref[...] = d_decay.astype(BF16)
    scale = width ** (-0.5)
    dq = (dq_unit - q * (q_norm * q_norm * jnp.sum(q * dq_unit, axis=1, keepdims=True))) * (q_norm * scale)
    dq_ref[...] = dq.astype(BF16)
    dk_unit = up + down
    dk = (dk_unit - k * (k_norm * k_norm * jnp.sum(k * dk_unit, axis=1, keepdims=True))) * k_norm
    dk_ref[...] = dk.astype(BF16)


def passed_along(value, axis, steps):
    count = lax.axis_size(axis)
    leading, last = (max(0, -steps), min(count, count - steps))
    return lax.ppermute(value, axis, [(source, source + steps) for source in range(leading, last)])


def relay(trans, ends, inject):
    n_context = lax.axis_size("ctx")

    def turn(turn_index, carried):
        leaving, back_leaving, _, _ = carried
        arriving = passed_along(leaving, "ctx", 1)
        back_arriving = passed_along(back_leaving, "ctx", -1)
        leaving = jnp.einsum("hab,hbc->hac", trans, arriving, precision=exact_prec) + ends
        back_leaving = jnp.einsum("hba,hbc->hac", trans, back_arriving, precision=exact_prec) + inject
        return (leaving, back_leaving, arriving, back_arriving)

    zero = jnp.zeros_like(ends)
    return lax.fori_loop(0, n_context - 1, turn, (ends, inject, zero, zero))[2:]


def per_device(queries, key_in, values_in, strength, log_decay, d_out):
    heads_all = strength.shape[1]
    heads = heads_all // lax.axis_size("head")
    width = queries.shape[1] // heads_all

    def gathered(array):
        return lax.all_to_all(array, "head", split_axis=1, concat_axis=0, tiled=True)

    k, g, s, q, v, o = (gathered(x) for x in (key_in, log_decay, strength, queries, values_in, d_out))
    s = s.astype(F32)
    rows = q.shape[0]
    spans = rows // SPAN
    token = pl.BlockSpec((rows, width), lambda h: (0, h))
    table = pl.BlockSpec((rows, heads), lambda h: (0, 0))
    narrow = pl.BlockSpec((1, rows, width), lambda h: (h, 0, 0))
    square = pl.BlockSpec((1, rows, rows), lambda h: (h, 0, 0))
    state = pl.BlockSpec((1, width, width), lambda h: (h, 0, 0))
    state_list = pl.BlockSpec((1, spans, width, width), lambda h: (h, 0, 0, 0))
    inputs = [token] * 5 + [table]
    narrow_t = jax.ShapeDtypeStruct((heads, rows, width), F32)
    square_t = jax.ShapeDtypeStruct((heads, rows, rows), F32)
    state_t = jax.ShapeDtypeStruct((heads, width, width), F32)
    state_list_t = jax.ShapeDtypeStruct((heads, spans, width, width), F32)
    token_t = jax.ShapeDtypeStruct((rows, heads * width), BF16)
    params = pltpu.CompilerParams(dimension_semantics=("arbitrary",), vmem_limit_bytes=40 * 1024 * 1024)
    saved_specs = [narrow] * 2 + [square] * 3 + [state_list] * 3
    saved_types = [narrow_t] * 2 + [square_t] * 3 + [state_list_t] * 3
    results = pl.pallas_call(
        functools.partial(local_kernel, SPAN),
        grid=(heads,),
        in_specs=inputs,
        out_specs=saved_specs + [state] * 3,
        out_shape=saved_types + [state_t] * 3,
        compiler_params=params,
        name="local_part",
    )(q, k, v, g, o, s)
    saved = results[:8]
    ends, trans, inject = results[8:]
    state_in, grad_in = relay(trans, ends, inject)
    dq, dk, dv, dg, ds = pl.pallas_call(
        functools.partial(grad_kernel, SPAN),
        grid=(heads,),
        in_specs=inputs + saved_specs + [state] * 2,
        out_specs=[token] * 4 + [table],
        out_shape=[token_t] * 4 + [jax.ShapeDtypeStruct((rows, heads), F32)],
        compiler_params=params,
        name="grad_part",
    )(q, k, v, g, o, s, *saved, state_in, grad_in)

    def returned(array):
        return lax.all_to_all(array, "head", split_axis=0, concat_axis=1, tiled=True)

    return (returned(dq), returned(dk), returned(dv), returned(ds.astype(BF16)), returned(dg))


def solution(mesh):
    spec = P(("ctx", "head"), None)
    return jax.shard_map(
        per_device, mesh=mesh, in_specs=(spec,) * 6, out_specs=(spec,) * 5, check_vma=False
    )
```

time: 758 us -> 419 us (0.55)
  the two profiles are of different devices: /device:TPU:4 before, /device:TPU:2 now
where the time goes in v1:
time: 419 us; the launch traced here: 417 us
  waiting for transfers between devices  140 us (33%)
  starting transfers between devices  74.2 us (18%)
  Pallas kernels  68.4 us (16%)
  blocking collectives  63 us (15%)
  matrix products  38.7 us (9%)
  local copies, waits for them, and re-layouts  32.2 us (8%)
    all_to_all x6, waiting for transfers between devices, gathered(): lax.all_to_all(array, 'head', split_axis=1, concat_axis=0, tiled=True)  69.2 us
    all_to_all x4, blocking collectives, returned(): lax.all_to_all(array, 'head', split_axis=0, concat_axis=1, tiled=True)  63 us
    ppermute x14, waiting for transfers between devices, passed_along(): lax.ppermute(value, axis, [(source, source + steps) for source in range(l...  59.6 us
    ppermute x14, starting transfers between devices, passed_along(): lax.ppermute(value, axis, [(source, source + steps) for source in range(l...  48.5 us
    pallas_call x1, Pallas kernels, per_device(): pl.pallas_call(functools.partial(local_kernel, SPAN), grid=(heads,), in_s...  41.7 us
    pallas_call x1, Pallas kernels, per_device(): pl.pallas_call(functools.partial(grad_kernel, SPAN), grid=(heads,), in_sp...  26.7 us
    all_to_all x6, starting transfers between devices, gathered(): lax.all_to_all(array, 'head', split_axis=1, concat_axis=0, tiled=True)  22.2 us
    unnamed x45, local copies, waits for them, and re-layouts  21.7 us
  transfers between devices with their start and end apart: 21, of which 21 were waited for; matrix products, arithmetic and copies ran while one was open for 7% of the time, Pallas kernels for 0%

profile of v1, /device:TPU:2, one launch (start us, length us, event | category | flops | bytes accessed | tf_op | source)
XLA Modules:
  0.0 417.2 jit_solution(5290451531983339675)
XLA Ops:
  2.0 4.9 %all-to-all-start.5 = ((bf16[4,2,256]{2,1,0:T(2,128)(2,1)}), bf16[4,2,256]{2,1,0:T(2,128)(2,1)S(1)}, u32[]{:S(2)}, u32[]{:S(2)}) async-start(bf16[4,2,256]{2,1,0:T(2,128)(2,1)} %reshape.46), calls=%async_computation.5 | async-start | bytes 8192 | tf_op jit(solution)/shard_map/all_to_all | solution.py:268
  8.8 3.6 all-to-all-done.5
  12.5 3.5 all-to-all-start
  16.8 12.4 %all-to-all-done = bf16[64,4,1024]{2,0,1:T(8,128)(2,1)S(1)} async-done(((bf16[64,4,1024]{2,0,1:T(8,128)(2,1)}), bf16[64,4,1024]{2,0,1:T(8,128)(2,1)S(1)}, u32[]{:S(2)}, u32[]{:S(2)}) %all-to-all-start) | async-done | bytes 524320 | tf_op jit(solution)/shard_map/all_to_all | solution.py:268
  29.3 3.5 all-to-all-start.1
  33.6 13.0 %all-to-all-done.1 = bf16[64,4,1024]{2,0,1:T(8,128)(2,1)S(1)} async-done(((bf16[64,4,1024]{2,0,1:T(8,128)(2,1)}), bf16[64,4,1024]{2,0,1:T(8,128)(2,1)S(1)}, u32[]{:S(2)}, u32[]{:S(2)}) %all-to-all-start.1) | async-done | bytes 524320 | tf_op jit(solution)/shard_map/all_to_all | solution.py:268
  46.6 3.5 all-to-all-start.2
  50.9 13.2 %all-to-all-done.2 = bf16[64,4,1024]{2,0,1:T(8,128)(2,1)S(1)} async-done(((bf16[64,4,1024]{2,0,1:T(8,128)(2,1)}), bf16[64,4,1024]{2,0,1:T(8,128)(2,1)S(1)}, u32[]{:S(2)}, u32[]{:S(2)}) %all-to-all-start.2) | async-done | bytes 524320 | tf_op jit(solution)/shard_map/all_to_all | solution.py:268
  64.1 3.5 all-to-all-start.3
  68.4 13.2 %all-to-all-done.3 = bf16[64,4,1024]{2,0,1:T(8,128)(2,1)S(1)} async-done(((bf16[64,4,1024]{2,0,1:T(8,128)(2,1)}), bf16[64,4,1024]{2,0,1:T(8,128)(2,1)S(1)}, u32[]{:S(2)}, u32[]{:S(2)}) %all-to-all-start.3) | async-done | bytes 524320 | tf_op jit(solution)/shard_map/all_to_all | solution.py:268
  81.6 3.5 all-to-all-start.4
  85.3 13.8 %all-to-all-done.4 = bf16[64,4,1024]{2,0,1:T(8,128)(2,1)S(1)} async-done(((bf16[64,4,1024]{2,0,1:T(8,128)(2,1)}), bf16[64,4,1024]{2,0,1:T(8,128)(2,1)S(1)}, u32[]{:S(2)}, u32[]{:S(2)}) %all-to-all-start.4) | async-done | bytes 524320 | tf_op jit(solution)/shard_map/all_to_all | solution.py:268
  99.1 41.7 %local_part.1 = (f32[8,256,128]{2,1,0:T(8,128)S(1)}, f32[8,256,128]{2,1,0:T(8,128)S(1)}, f32[8,256,256]{2,1,0:T(8,128)S(1)}, f32[8,256,256]{2,1,0:T(8,128)S(1)},...) custom-call(bf16[256,1024]{1,0:T(8,128)(2,1)S(1)} %bitcast.80, ...), custom_call_target="tpu_custom_call" | custom-call | tf_op jit(solution)/shard_map/local_part/pallas_call | solution.py:289
  153.1 147.0 %while.16 = (s32[]{:T(128)}, f32[8,128,128]{2,1,0:T(8,128)}, f32[8,128,128]{2,1,0:T(8,128)}, f32[8,128,128]{2,1,0:T(8,128)}, f32[8,128,128]{2,1,0:T(8,128)}, /*i...) while((s32[]{:T(128)}, f32[8,128,128]{2,1,0:T(8,128)}, ...), condition=%wide.region_1.0_spmd, body=%wide.region_0.0_spmd.sunk | while | flops 402915328 | bytes 10485961 | solution.py:259
  155.0 3.6 collective-permute-start.1
  158.7 5.2 %collective-permute-done = f32[8,128,128]{2,1,0:T(8,128)} collective-permute-done((f32[8,128,128]{2,1,0:T(8,128)}, f32[8,128,128]{2,1,0:T(8,128)}, u32[]{:S(2)}, u32[]{:S(2)}) %collective-permute-start) | collective-permute-done | bytes 524320 | tf_op jit(solution)/shard_map/while/body/eval_jaxpr/ppermute | solution.py:244
  163.9 3.0 convolution_add_fusion.4
  171.0 3.7 collective-permute-start
  176.8 5.2 %collective-permute-done = f32[8,128,128]{2,1,0:T(8,128)} collective-permute-done((f32[8,128,128]{2,1,0:T(8,128)}, f32[8,128,128]{2,1,0:T(8,128)}, u32[]{:S(2)}, u32[]{:S(2)}) %collective-permute-start) | collective-permute-done | bytes 524320 | tf_op jit(solution)/shard_map/while/body/eval_jaxpr/ppermute | solution.py:244
  182.0 3.0 convolution_add_fusion.4
  185.0 3.6 collective-permute-done.1
  191.1 4.3 %collective-permute-start = (f32[8,128,128]{2,1,0:T(8,128)}, f32[8,128,128]{2,1,0:T(8,128)}, u32[]{:S(2)}, u32[]{:S(2)}) collective-permute-start(f32[8,128,128]{2,1,0:T(8,128)} %get-tuple-element.167), channel_id=1, source_target_pairs={{0,4},{4,8},{8,12},{12,16},{16,20},{20,24},{24,28},{1,5},{5,9},{9,... | collective-permute-start | bytes 1572872 | tf_op jit(solution)/shard_map/while/body/eval_jaxpr/ppermute | solution.py:244
  197.4 4.7 %collective-permute-done = f32[8,128,128]{2,1,0:T(8,128)} collective-permute-done((f32[8,128,128]{2,1,0:T(8,128)}, f32[8,128,128]{2,1,0:T(8,128)}, u32[]{:S(2)}, u32[]{:S(2)}) %collective-permute-start) | collective-permute-done | bytes 524320 | tf_op jit(solution)/shard_map/while/body/eval_jaxpr/ppermute | solution.py:244
  202.1 3.0 convolution_add_fusion.4
  205.1 4.1 collective-permute-done.1
  211.7 5.8 %collective-permute-start = (f32[8,128,128]{2,1,0:T(8,128)}, f32[8,128,128]{2,1,0:T(8,128)}, u32[]{:S(2)}, u32[]{:S(2)}) collective-permute-start(f32[8,128,128]{2,1,0:T(8,128)} %get-tuple-element.167), channel_id=1, source_target_pairs={{0,4},{4,8},{8,12},{12,16},{16,20},{20,24},{24,28},{1,5},{5,9},{9,... | collective-permute-start | bytes 1572872 | tf_op jit(solution)/shard_map/while/body/eval_jaxpr/ppermute | solution.py:244
  219.5 3.2 collective-permute-done
  222.7 3.0 convolution_add_fusion.4
  225.7 5.6 %collective-permute-done.1 = f32[8,128,128]{2,1,0:T(8,128)} collective-permute-done((f32[8,128,128]{2,1,0:T(8,128)}, f32[8,128,128]{2,1,0:T(8,128)}, u32[]{:S(2)}, u32[]{:S(2)}) %collective-permute-start.1) | collective-permute-done | bytes 524320 | tf_op jit(solution)/shard_map/while/body/eval_jaxpr/ppermute | solution.py:244
  233.8 5.8 %collective-permute-start = (f32[8,128,128]{2,1,0:T(8,128)}, f32[8,128,128]{2,1,0:T(8,128)}, u32[]{:S(2)}, u32[]{:S(2)}) collective-permute-start(f32[8,128,128]{2,1,0:T(8,128)} %get-tuple-element.167), channel_id=1, source_target_pairs={{0,4},{4,8},{8,12},{12,16},{16,20},{20,24},{24,28},{1,5},{5,9},{9,... | collective-permute-start | bytes 1572872 | tf_op jit(solution)/shard_map/while/body/eval_jaxpr/ppermute | solution.py:244
  241.6 3.2 collective-permute-done
  244.8 3.0 convolution_add_fusion.4
  247.8 5.6 %collective-permute-done.1 = f32[8,128,128]{2,1,0:T(8,128)} collective-permute-done((f32[8,128,128]{2,1,0:T(8,128)}, f32[8,128,128]{2,1,0:T(8,128)}, u32[]{:S(2)}, u32[]{:S(2)}) %collective-permute-start.1) | collective-permute-done | bytes 524320 | tf_op jit(solution)/shard_map/while/body/eval_jaxpr/ppermute | solution.py:244
  255.9 5.8 %collective-permute-start = (f32[8,128,128]{2,1,0:T(8,128)}, f32[8,128,128]{2,1,0:T(8,128)}, u32[]{:S(2)}, u32[]{:S(2)}) collective-permute-start(f32[8,128,128]{2,1,0:T(8,128)} %get-tuple-element.167), channel_id=1, source_target_pairs={{0,4},{4,8},{8,12},{12,16},{16,20},{20,24},{24,28},{1,5},{5,9},{9,... | collective-permute-start | bytes 1572872 | tf_op jit(solution)/shard_map/while/body/eval_jaxpr/ppermute | solution.py:244
  263.7 3.2 collective-permute-done
  266.9 3.0 convolution_add_fusion.4
  269.9 5.6 %collective-permute-done.1 = f32[8,128,128]{2,1,0:T(8,128)} collective-permute-done((f32[8,128,128]{2,1,0:T(8,128)}, f32[8,128,128]{2,1,0:T(8,128)}, u32[]{:S(2)}, u32[]{:S(2)}) %collective-permute-start.1) | collective-permute-done | bytes 524320 | tf_op jit(solution)/shard_map/while/body/eval_jaxpr/ppermute | solution.py:244
  278.0 5.8 %collective-permute-start = (f32[8,128,128]{2,1,0:T(8,128)}, f32[8,128,128]{2,1,0:T(8,128)}, u32[]{:S(2)}, u32[]{:S(2)}) collective-permute-start(f32[8,128,128]{2,1,0:T(8,128)} %get-tuple-element.167), channel_id=1, source_target_pairs={{0,4},{4,8},{8,12},{12,16},{16,20},{20,24},{24,28},{1,5},{5,9},{9,... | collective-permute-start | bytes 1572872 | tf_op jit(solution)/shard_map/while/body/eval_jaxpr/ppermute | solution.py:244
  285.8 3.2 collective-permute-done
  289.0 3.0 convolution_add_fusion.4
  292.0 5.6 %collective-permute-done.1 = f32[8,128,128]{2,1,0:T(8,128)} collective-permute-done((f32[8,128,128]{2,1,0:T(8,128)}, f32[8,128,128]{2,1,0:T(8,128)}, u32[]{:S(2)}, u32[]{:S(2)}) %collective-permute-start.1) | collective-permute-done | bytes 524320 | tf_op jit(solution)/shard_map/while/body/eval_jaxpr/ppermute | solution.py:244
  307.3 26.7 %grad_part.1 = (bf16[256,1024]{1,0:T(8,128)(2,1)S(1)}, bf16[256,1024]{1,0:T(8,128)(2,1)S(1)}, bf16[256,1024]{1,0:T(8,128)(2,1)S(1)}, bf16[256,1024]{1,0:T(8,128)(2,1)}, f32[256,8]{1,0:T(8,128)S(1)}) custom-call(bf16[256,1024]{1,0:T(8,128)(2,1)S(1)} %bitcast.81, bf16[256,1024]{1,0:T(8,128)(2,1)S(1)} %bitcast.83, bf16[256,1024]{1,0:T(8,128)(2,1)S(1)} %bitcast.85, ...), custom_call_target="tpu_custom_call" | custom-call | tf_op jit(solution)/shard_map/grad_part/pallas_call | solution.py:301
  335.8 8.1 %all_to_all.203 = bf16[4,2,256]{2,1,0:T(2,128)(2,1)S(1)} all-to-all(bf16[4,2,256]{2,1,0:T(2,128)(2,1)S(1)} %reshape.48), channel_id=1, replica_groups=mesh['ctx'=8,'head'=4] {'head'}, dimensions={0} | all-to-all | bytes 8192 | tf_op jit(solution)/shard_map/all_to_all | solution.py:312
  343.9 18.1 %all_to_all.204 = bf16[4,64,1024]{2,1,0:T(8,128)(2,1)S(1)} all-to-all(bf16[4,64,1024]{2,1,0:T(8,128)(2,1)} %bitcast.94), channel_id=1, replica_groups=mesh['ctx'=8,'head'=4] {'head'}, dimensions={0} | all-to-all | bytes 1048576 | tf_op jit(solution)/shard_map/all_to_all | solution.py:312
  362.0 19.3 %all_to_all.205 = bf16[4,64,1024]{2,1,0:T(8,128)(2,1)S(1)} all-to-all(bf16[4,64,1024]{2,1,0:T(8,128)(2,1)} %bitcast.93), channel_id=1, replica_groups=mesh['ctx'=8,'head'=4] {'head'}, dimensions={0} | all-to-all | bytes 1048576 | tf_op jit(solution)/shard_map/all_to_all | solution.py:312
  381.3 17.4 %all_to_all.206 = bf16[4,64,1024]{2,1,0:T(8,128)(2,1)S(1)} all-to-all(bf16[4,64,1024]{2,1,0:T(8,128)(2,1)S(1)} %bitcast.92), channel_id=1, replica_groups=mesh['ctx'=8,'head'=4] {'head'}, dimensions={0} | all-to-all | bytes 1048576 | tf_op jit(solution)/shard_map/all_to_all | solution.py:312
  398.8 3.5 all-to-all-start.10
  405.5 10.9 %all-to-all-done.10 = bf16[4,64,1024]{2,1,0:T(8,128)(2,1)S(1)} async-done(((bf16[4,64,1024]{2,1,0:T(8,128)(2,1)}), bf16[4,64,1024]{2,1,0:T(8,128)(2,1)S(1)}, u32[]{:S(2)}, u32[]{:S(2)}) %all-to-all-start.10) | async-done | bytes 524320 | tf_op jit(solution)/shard_map/all_to_all | solution.py:312
  (91 shorter events, 64.7 us)
Async XLA Ops:
  0.6 0.7 copy-start
  0.6 15.3 %copy-start.16 = (bf16[64,4096]{1,0:T(8,128)(2,1)S(1)}, bf16[64,4096]{1,0:T(8,128)(2,1)}, u32[]{:S(2)}) copy-start(bf16[64,4096]{1,0:T(8,128)(2,1)} %param.9) | copy-start | bytes 1572868
  2.0 10.5 %all-to-all-start.5 = ((bf16[4,2,256]{2,1,0:T(2,128)(2,1)}), bf16[4,2,256]{2,1,0:T(2,128)(2,1)S(1)}, u32[]{:S(2)}, u32[]{:S(2)}) async-start(bf16[4,2,256]{2,1,0:T(2,128)(2,1)} %reshape.46), calls=%async_computation.5 | async-start | bytes 8192 | tf_op jit(solution)/shard_map/all_to_all | solution.py:268
  6.9 25.8 %copy-start.17 = (bf16[64,4096]{1,0:T(8,128)(2,1)S(1)}, bf16[64,4096]{1,0:T(8,128)(2,1)}, u32[]{:S(2)}) copy-start(bf16[64,4096]{1,0:T(8,128)(2,1)} %param.10) | copy-start | bytes 1572868
  12.5 16.8 %all-to-all-start = ((bf16[64,4,1024]{2,0,1:T(8,128)(2,1)}), bf16[64,4,1024]{2,0,1:T(8,128)(2,1)S(1)}, u32[]{:S(2)}, u32[]{:S(2)}) async-start(bf16[64,4,1024]{2,0,1:T(8,128)(2,1)} %bitcast.71), calls=%async_computation | async-start | bytes 1048576 | tf_op jit(solution)/shard_map/all_to_all | solution.py:268
  16.0 34.1 %copy-start.18 = (bf16[64,4096]{1,0:T(8,128)(2,1)S(1)}, bf16[64,4096]{1,0:T(8,128)(2,1)}, u32[]{:S(2)}) copy-start(bf16[64,4096]{1,0:T(8,128)(2,1)} %param.12) | copy-start | bytes 1572868
  29.3 17.3 %all-to-all-start.1 = ((bf16[64,4,1024]{2,0,1:T(8,128)(2,1)}), bf16[64,4,1024]{2,0,1:T(8,128)(2,1)S(1)}, u32[]{:S(2)}, u32[]{:S(2)}) async-start(bf16[64,4,1024]{2,0,1:T(8,128)(2,1)} %bitcast.70), calls=%async_computation.1 | async-start | bytes 1048576 | tf_op jit(solution)/shard_map/all_to_all | solution.py:268
  32.7 34.8 %copy-start.19 = (bf16[64,4096]{1,0:T(8,128)(2,1)S(1)}, bf16[64,4096]{1,0:T(8,128)(2,1)}, u32[]{:S(2)}) copy-start(bf16[64,4096]{1,0:T(8,128)(2,1)} %param.13) | copy-start | bytes 1572868
  46.6 17.5 %all-to-all-start.2 = ((bf16[64,4,1024]{2,0,1:T(8,128)(2,1)}), bf16[64,4,1024]{2,0,1:T(8,128)(2,1)S(1)}, u32[]{:S(2)}, u32[]{:S(2)}) async-start(bf16[64,4,1024]{2,0,1:T(8,128)(2,1)} %bitcast.69), calls=%async_computation.2 | async-start | bytes 1048576 | tf_op jit(solution)/shard_map/all_to_all | solution.py:268
  64.1 17.5 %all-to-all-start.3 = ((bf16[64,4,1024]{2,0,1:T(8,128)(2,1)}), bf16[64,4,1024]{2,0,1:T(8,128)(2,1)S(1)}, u32[]{:S(2)}, u32[]{:S(2)}) async-start(bf16[64,4,1024]{2,0,1:T(8,128)(2,1)} %bitcast.68), calls=%async_computation.3 | async-start | bytes 1048576 | tf_op jit(solution)/shard_map/all_to_all | solution.py:268
  81.6 17.5 %all-to-all-start.4 = ((bf16[64,4,1024]{2,0,1:T(8,128)(2,1)}), bf16[64,4,1024]{2,0,1:T(8,128)(2,1)S(1)}, u32[]{:S(2)}, u32[]{:S(2)}) async-start(bf16[64,4,1024]{2,0,1:T(8,128)(2,1)} %bitcast.67), calls=%async_computation.4 | async-start | bytes 1048576 | tf_op jit(solution)/shard_map/all_to_all | solution.py:268
  140.8 1.4 copy-start.1
  142.2 1.4 copy-start.3
  143.6 1.4 copy-start.5
  144.9 1.4 copy-start.7
  146.3 1.0 copy-start.8
  147.3 1.0 copy-start.10
  149.3 3.8 copy-start.14
  153.1 10.8 %collective-permute-start = (f32[8,128,128]{2,1,0:T(8,128)}, f32[8,128,128]{2,1,0:T(8,128)}, u32[]{:S(2)}, u32[]{:S(2)}) collective-permute-start(f32[8,128,128]{2,1,0:T(8,128)} %get-tuple-element.167), channel_id=1, source_target_pairs={{0,4},{4,8},{8,12},{12,16},{16,20},{20,24},{24,28},{1,5},{5,9},{9,... | collective-permute-start | bytes 1572872 | tf_op jit(solution)/shard_map/while/body/eval_jaxpr/ppermute | solution.py:244
  155.0 13.5 %collective-permute-start.1 = (f32[8,128,128]{2,1,0:T(8,128)}, f32[8,128,128]{2,1,0:T(8,128)}, u32[]{:S(2)}, u32[]{:S(2)}) collective-permute-start(f32[8,128,128]{2,1,0:T(8,128)} %get-tuple-element.168), channel_id=1, source_target_pairs={{4,0},{8,4},{12,8},{16,12},{20,16},{24,20},{28,24},{5,1},{9,5},{13... | collective-permute-start | bytes 1572872 | tf_op jit(solution)/shard_map/while/body/eval_jaxpr/ppermute | solution.py:244
  158.7 9.9 %copy-start.15 = (f32[8,128,128]{2,1,0:T(8,128)S(1)}, f32[8,128,128]{2,1,0:T(8,128)}, u32[]{:S(2)}) copy-start(f32[8,128,128]{2,1,0:T(8,128)} %get-tuple-element.182) | copy-start | bytes 1572868 | tf_op jit(solution)/shard_map/while
  171.0 11.0 %collective-permute-start = (f32[8,128,128]{2,1,0:T(8,128)}, f32[8,128,128]{2,1,0:T(8,128)}, u32[]{:S(2)}, u32[]{:S(2)}) collective-permute-start(f32[8,128,128]{2,1,0:T(8,128)} %get-tuple-element.167), channel_id=1, source_target_pairs={{0,4},{4,8},{8,12},{12,16},{16,20},{20,24},{24,28},{1,5},{5,9},{9,... | collective-permute-start | bytes 1572872 | tf_op jit(solution)/shard_map/while/body/eval_jaxpr/ppermute | solution.py:244
  174.7 13.9 %collective-permute-start.1 = (f32[8,128,128]{2,1,0:T(8,128)}, f32[8,128,128]{2,1,0:T(8,128)}, u32[]{:S(2)}, u32[]{:S(2)}) collective-permute-start(f32[8,128,128]{2,1,0:T(8,128)} %get-tuple-element.168), channel_id=1, source_target_pairs={{4,0},{8,4},{12,8},{16,12},{20,16},{24,20},{28,24},{5,1},{9,5},{13... | collective-permute-start | bytes 1572872 | tf_op jit(solution)/shard_map/while/body/eval_jaxpr/ppermute | solution.py:244
  176.8 11.9 %copy-start.15 = (f32[8,128,128]{2,1,0:T(8,128)S(1)}, f32[8,128,128]{2,1,0:T(8,128)}, u32[]{:S(2)}) copy-start(f32[8,128,128]{2,1,0:T(8,128)} %get-tuple-element.182) | copy-start | bytes 1572868 | tf_op jit(solution)/shard_map/while
  191.1 11.0 %collective-permute-start = (f32[8,128,128]{2,1,0:T(8,128)}, f32[8,128,128]{2,1,0:T(8,128)}, u32[]{:S(2)}, u32[]{:S(2)}) collective-permute-start(f32[8,128,128]{2,1,0:T(8,128)} %get-tuple-element.167), channel_id=1, source_target_pairs={{0,4},{4,8},{8,12},{12,16},{16,20},{20,24},{24,28},{1,5},{5,9},{9,... | collective-permute-start | bytes 1572872 | tf_op jit(solution)/shard_map/while/body/eval_jaxpr/ppermute | solution.py:244
  195.4 13.8 %collective-permute-start.1 = (f32[8,128,128]{2,1,0:T(8,128)}, f32[8,128,128]{2,1,0:T(8,128)}, u32[]{:S(2)}, u32[]{:S(2)}) collective-permute-start(f32[8,128,128]{2,1,0:T(8,128)} %get-tuple-element.168), channel_id=1, source_target_pairs={{4,0},{8,4},{12,8},{16,12},{20,16},{24,20},{28,24},{5,1},{9,5},{13... | collective-permute-start | bytes 1572872 | tf_op jit(solution)/shard_map/while/body/eval_jaxpr/ppermute | solution.py:244
  197.4 11.9 %copy-start.15 = (f32[8,128,128]{2,1,0:T(8,128)S(1)}, f32[8,128,128]{2,1,0:T(8,128)}, u32[]{:S(2)}) copy-start(f32[8,128,128]{2,1,0:T(8,128)} %get-tuple-element.182) | copy-start | bytes 1572868 | tf_op jit(solution)/shard_map/while
  211.7 11.0 %collective-permute-start = (f32[8,128,128]{2,1,0:T(8,128)}, f32[8,128,128]{2,1,0:T(8,128)}, u32[]{:S(2)}, u32[]{:S(2)}) collective-permute-start(f32[8,128,128]{2,1,0:T(8,128)} %get-tuple-element.167), channel_id=1, source_target_pairs={{0,4},{4,8},{8,12},{12,16},{16,20},{20,24},{24,28},{1,5},{5,9},{9,... | collective-permute-start | bytes 1572872 | tf_op jit(solution)/shard_map/while/body/eval_jaxpr/ppermute | solution.py:244
  217.5 13.8 %collective-permute-start.1 = (f32[8,128,128]{2,1,0:T(8,128)}, f32[8,128,128]{2,1,0:T(8,128)}, u32[]{:S(2)}, u32[]{:S(2)}) collective-permute-start(f32[8,128,128]{2,1,0:T(8,128)} %get-tuple-element.168), channel_id=1, source_target_pairs={{4,0},{8,4},{12,8},{16,12},{20,16},{24,20},{28,24},{5,1},{9,5},{13... | collective-permute-start | bytes 1572872 | tf_op jit(solution)/shard_map/while/body/eval_jaxpr/ppermute | solution.py:244
  219.5 11.9 %copy-start.15 = (f32[8,128,128]{2,1,0:T(8,128)S(1)}, f32[8,128,128]{2,1,0:T(8,128)}, u32[]{:S(2)}) copy-start(f32[8,128,128]{2,1,0:T(8,128)} %get-tuple-element.182) | copy-start | bytes 1572868 | tf_op jit(solution)/shard_map/while
  233.8 11.0 %collective-permute-start = (f32[8,128,128]{2,1,0:T(8,128)}, f32[8,128,128]{2,1,0:T(8,128)}, u32[]{:S(2)}, u32[]{:S(2)}) collective-permute-start(f32[8,128,128]{2,1,0:T(8,128)} %get-tuple-element.167), channel_id=1, source_target_pairs={{0,4},{4,8},{8,12},{12,16},{16,20},{20,24},{24,28},{1,5},{5,9},{9,... | collective-permute-start | bytes 1572872 | tf_op jit(solution)/shard_map/while/body/eval_jaxpr/ppermute | solution.py:244
  239.6 13.8 %collective-permute-start.1 = (f32[8,128,128]{2,1,0:T(8,128)}, f32[8,128,128]{2,1,0:T(8,128)}, u32[]{:S(2)}, u32[]{:S(2)}) collective-permute-start(f32[8,128,128]{2,1,0:T(8,128)} %get-tuple-element.168), channel_id=1, source_target_pairs={{4,0},{8,4},{12,8},{16,12},{20,16},{24,20},{28,24},{5,1},{9,5},{13... | collective-permute-start | bytes 1572872 | tf_op jit(solution)/shard_map/while/body/eval_jaxpr/ppermute | solution.py:244
  241.6 11.9 %copy-start.15 = (f32[8,128,128]{2,1,0:T(8,128)S(1)}, f32[8,128,128]{2,1,0:T(8,128)}, u32[]{:S(2)}) copy-start(f32[8,128,128]{2,1,0:T(8,128)} %get-tuple-element.182) | copy-start | bytes 1572868 | tf_op jit(solution)/shard_map/while
  255.9 11.0 %collective-permute-start = (f32[8,128,128]{2,1,0:T(8,128)}, f32[8,128,128]{2,1,0:T(8,128)}, u32[]{:S(2)}, u32[]{:S(2)}) collective-permute-start(f32[8,128,128]{2,1,0:T(8,128)} %get-tuple-element.167), channel_id=1, source_target_pairs={{0,4},{4,8},{8,12},{12,16},{16,20},{20,24},{24,28},{1,5},{5,9},{9,... | collective-permute-start | bytes 1572872 | tf_op jit(solution)/shard_map/while/body/eval_jaxpr/ppermute | solution.py:244
  261.7 13.8 %collective-permute-start.1 = (f32[8,128,128]{2,1,0:T(8,128)}, f32[8,128,128]{2,1,0:T(8,128)}, u32[]{:S(2)}, u32[]{:S(2)}) collective-permute-start(f32[8,128,128]{2,1,0:T(8,128)} %get-tuple-element.168), channel_id=1, source_target_pairs={{4,0},{8,4},{12,8},{16,12},{20,16},{24,20},{28,24},{5,1},{9,5},{13... | collective-permute-start | bytes 1572872 | tf_op jit(solution)/shard_map/while/body/eval_jaxpr/ppermute | solution.py:244
  263.7 11.9 %copy-start.15 = (f32[8,128,128]{2,1,0:T(8,128)S(1)}, f32[8,128,128]{2,1,0:T(8,128)}, u32[]{:S(2)}) copy-start(f32[8,128,128]{2,1,0:T(8,128)} %get-tuple-element.182) | copy-start | bytes 1572868 | tf_op jit(solution)/shard_map/while
  278.0 11.0 %collective-permute-start = (f32[8,128,128]{2,1,0:T(8,128)}, f32[8,128,128]{2,1,0:T(8,128)}, u32[]{:S(2)}, u32[]{:S(2)}) collective-permute-start(f32[8,128,128]{2,1,0:T(8,128)} %get-tuple-element.167), channel_id=1, source_target_pairs={{0,4},{4,8},{8,12},{12,16},{16,20},{20,24},{24,28},{1,5},{5,9},{9,... | collective-permute-start | bytes 1572872 | tf_op jit(solution)/shard_map/while/body/eval_jaxpr/ppermute | solution.py:244
  283.8 13.8 %collective-permute-start.1 = (f32[8,128,128]{2,1,0:T(8,128)}, f32[8,128,128]{2,1,0:T(8,128)}, u32[]{:S(2)}, u32[]{:S(2)}) collective-permute-start(f32[8,128,128]{2,1,0:T(8,128)} %get-tuple-element.168), channel_id=1, source_target_pairs={{4,0},{8,4},{12,8},{16,12},{20,16},{24,20},{28,24},{5,1},{9,5},{13... | collective-permute-start | bytes 1572872 | tf_op jit(solution)/shard_map/while/body/eval_jaxpr/ppermute | solution.py:244
  285.8 11.9 %copy-start.15 = (f32[8,128,128]{2,1,0:T(8,128)S(1)}, f32[8,128,128]{2,1,0:T(8,128)}, u32[]{:S(2)}) copy-start(f32[8,128,128]{2,1,0:T(8,128)} %get-tuple-element.182) | copy-start | bytes 1572868 | tf_op jit(solution)/shard_map/while
  300.1 1.6 copy-start.2
  301.7 1.6 copy-start.4
  303.3 1.6 copy-start.6
  304.9 1.2 copy-start.9
  306.1 1.2 copy-start.11
  334.0 0.8 copy-start.12
  334.8 0.8 copy-start.13
  398.8 17.6 %all-to-all-start.10 = ((bf16[4,64,1024]{2,1,0:T(8,128)(2,1)}), bf16[4,64,1024]{2,1,0:T(8,128)(2,1)S(1)}, u32[]{:S(2)}, u32[]{:S(2)}) async-start(bf16[4,64,1024]{2,1,0:T(8,128)(2,1)} %bitcast.27), calls=%async_computation.10 | async-start | bytes 1048576 | tf_op jit(solution)/shard_map/all_to_all | solution.py:312

commit v2 on v1

--- a/solution.py
+++ b/solution.py
@@ -12,7 +12,7 @@
 EPS = 1e-06
 F32 = jnp.float32
 BF16 = jnp.bfloat16
-exact_prec = lax.Precision.HIGHEST
+MESH = pl.DeviceIdType.MESH
 
 NN = (((1,), (0,)), ((), ()))
 NT = (((1,), (1,)), ((), ()))
@@ -238,25 +238,170 @@
     dk_ref[...] = dk.astype(BF16)
 
 
-def passed_along(value, axis, steps):
-    count = lax.axis_size(axis)
-    leading, last = (max(0, -steps), min(count, count - steps))
-    return lax.ppermute(value, axis, [(source, source + steps) for source in range(leading, last)])
+def relay_kernel(n, trans_ref, end_ref, inject_ref, state_ref, grad_ref, move_ref, turn_ref, in_f, in_b, out_f, out_b,
+                 recv_f, recv_b, send_f, send_b):
+    me = lax.axis_index("ctx")
+    heads = trans_ref.shape[0]
+    first, last = me == 0, me == n - 1
+    barrier = pltpu.get_barrier_semaphore()
+
+    def push(out, arrive, send, recv, h, target):
+        return pltpu.make_async_remote_copy(
+            src_ref=out.at[h], dst_ref=arrive.at[h], send_sem=send.at[h], recv_sem=recv.at[h],
+            device_id={"ctx": target}, device_id_type=MESH,
+        )
+
+    @pl.when(jnp.logical_not(first))
+    def _():
+        pl.semaphore_signal(barrier, inc=1, device_id={"ctx": me - 1}, device_id_type=MESH)
+
+    @pl.when(jnp.logical_not(last))
+    def _():
+        pl.semaphore_signal(barrier, inc=1, device_id={"ctx": me + 1}, device_id_type=MESH)
+
+    @pl.when(first)
+    def _():
+        in_f[...] = jnp.zeros_like(in_f)
+
+    @pl.when(last)
+    def _():
+        in_b[...] = jnp.zeros_like(in_b)
+
+    for h in range(heads):
+        trans = trans_ref[h]
+        move_ref[0, h], move_ref[1, h] = split(trans)
+        turn_ref[0, h], turn_ref[1, h] = split(trans.T)
+
+    @pl.when(first | last)
+    def _():
+        pl.semaphore_wait(barrier, 1)
+
+    @pl.when(jnp.logical_not(first | last))
+    def _():
+        pl.semaphore_wait(barrier, 2)
+
+    def forward(h):
+        @pl.when(jnp.logical_not(first))
+        def _():
+            push(out_f, in_f, send_f, recv_f, h, me - 1).wait_recv()
+
+        state = in_f[h]
+        state_ref[h] = state
+
+        @pl.when(jnp.logical_not(last))
+        def _():
+            out_f[h] = dot3((move_ref[0, h], move_ref[1, h]), split(state)) + end_ref[h]
+            push(out_f, in_f, send_f, recv_f, h, me + 1).start()
+
+    def backward(h):
+        @pl.when(jnp.logical_not(last))
+        def _():
+            push(out_b, in_b, send_b, recv_b, h, me + 1).wait_recv()
+
+        grad = in_b[h]
+        grad_ref[h] = grad
+
+        @pl.when(jnp.logical_not(first))
+        def _():
+            out_b[h] = dot3((turn_ref[0, h], turn_ref[1, h]), split(grad)) + inject_ref[h]
+            push(out_b, in_b, send_b, recv_b, h, me - 1).start()
+
+    early = 2 * me < n
+    middle = (2 * me == n - 2) | (2 * me == n)
+    lag = jnp.where(middle, min(3, heads), heads)
+    lag_f = jnp.where(early, 0, lag)
+    lag_b = jnp.where(early, lag, 0)
+
+    def step(t, carry):
+        @pl.when((t >= lag_f) & (t < lag_f + heads))
+        def _():
+            forward(t - lag_f)
+
+        @pl.when((t >= lag_b) & (t < lag_b + heads))
+        def _():
+            backward(t - lag_b)
+
+        return carry
+
+    lax.fori_loop(0, 2 * heads, step, 0)
+
+    def finish(h, carry):
+        @pl.when(jnp.logical_not(last))
+        def _():
+            push(out_f, in_f, send_f, recv_f, h, me + 1).wait_send()
+
+        @pl.when(jnp.logical_not(first))
+        def _():
+            push(out_b, in_b, send_b, recv_b, h, me - 1).wait_send()
+
+        return carry
+
+    lax.fori_loop(0, heads, finish, 0)
 
 
 def relay(trans, ends, inject):
-    n_context = lax.axis_size("ctx")
-
-    def turn(turn_index, carried):
-        leaving, back_leaving, _, _ = carried
-        arriving = passed_along(leaving, "ctx", 1)
-        back_arriving = passed_along(back_leaving, "ctx", -1)
-        leaving = jnp.einsum("hab,hbc->hac", trans, arriving, precision=exact_prec) + ends
-        back_leaving = jnp.einsum("hba,hbc->hac", trans, back_arriving, precision=exact_prec) + inject
-        return (leaving, back_leaving, arriving, back_arriving)
-
-    zero = jnp.zeros_like(ends)
-    return lax.fori_loop(0, n_context - 1, turn, (ends, inject, zero, zero))[2:]
+    heads, width = trans.shape[:2]
+    whole = pl.BlockSpec(memory_space=pltpu.VMEM)
+    state_t = jax.ShapeDtypeStruct((heads, width, width), F32)
+    held = pltpu.VMEM((heads, width, width), F32)
+    halves = pltpu.VMEM((2, heads, width, width), BF16)
+    return pl.pallas_call(
+        functools.partial(relay_kernel, lax.axis_size("ctx")),
+        in_specs=[whole] * 3,
+        out_specs=[whole] * 2,
+        out_shape=[state_t] * 2,
+        scratch_shapes=[halves] * 2 + [held] * 4 + [pltpu.SemaphoreType.DMA((heads,))] * 4,
+        compiler_params=pltpu.CompilerParams(
+            collective_id=0, has_side_effects=True, vmem_limit_bytes=40 * 1024 * 1024
+        ),
+        name="relay",
+    )(trans, ends, inject)
+
+
+def exchange_kernel(n, count, source, target, *refs):
+    ins, outs = refs[:count], refs[count : 2 * count]
+    send, recv, own = refs[2 * count :]
+    me = lax.axis_index("head")
+    barrier = pltpu.get_barrier_semaphore()
+    for step in range(1, n):
+        pl.semaphore_signal(
+            barrier, inc=1, device_id={"head": lax.rem(me + step, n)}, device_id_type=MESH
+        )
+    local = [
+        pltpu.make_async_copy(source(i, a, me), target(i, b, me), own.at[i])
+        for i, (a, b) in enumerate(zip(ins, outs))
+    ]
+    for copy in local:
+        copy.start()
+    pl.semaphore_wait(barrier, n - 1)
+    copies = []
+    for i, (a, b) in enumerate(zip(ins, outs)):
+        for step in range(1, n):
+            peer = lax.rem(me + step, n)
+            copy = pltpu.make_async_remote_copy(
+                src_ref=source(i, a, peer), dst_ref=target(i, b, me), send_sem=send.at[i, step],
+                recv_sem=recv.at[i, step], device_id={"head": peer}, device_id_type=MESH,
+            )
+            copy.start()
+            copies.append(copy)
+    for copy in local + copies:
+        copy.wait()
+
+
+def exchange(arrays, types, source, target, identity, name):
+    count, n = len(arrays), lax.axis_size("head")
+    whole = pl.BlockSpec(memory_space=pltpu.VMEM)
+    return pl.pallas_call(
+        functools.partial(exchange_kernel, n, count, source, target),
+        in_specs=[whole] * count,
+        out_specs=[whole] * count,
+        out_shape=types,
+        scratch_shapes=[pltpu.SemaphoreType.DMA((count, n))] * 2 + [pltpu.SemaphoreType.DMA((count,))],
+        compiler_params=pltpu.CompilerParams(
+            collective_id=identity, has_side_effects=True, vmem_limit_bytes=40 * 1024 * 1024
+        ),
+        name=name,
+    )(*arrays)
 
 
 def per_device(queries, key_in, values_in, strength, log_decay, d_out):
@@ -264,10 +409,25 @@
     heads = heads_all // lax.axis_size("head")
     width = queries.shape[1] // heads_all
 
-    def gathered(array):
-        return lax.all_to_all(array, "head", split_axis=1, concat_axis=0, tiled=True)
-
-    k, g, s, q, v, o = (gathered(x) for x in (key_in, log_decay, strength, queries, values_in, d_out))
+    n = lax.axis_size("head")
+    share = queries.shape[0]
+    local_width = heads * width
+
+    def columns(index, ref, peer):
+        if index == 5:
+            return ref
+        return ref.at[:, pl.ds(pl.multiple_of(peer * local_width, local_width), local_width)]
+
+    def tokens(index, ref, peer):
+        return ref.at[pl.ds(pl.multiple_of(peer * share, share), share)]
+
+    k, g, q, v, o, s = exchange(
+        (key_in, log_decay, queries, values_in, d_out, strength),
+        [jax.ShapeDtypeStruct((n * share, local_width), BF16)] * 5
+        + [jax.ShapeDtypeStruct((n * share, heads_all), BF16)],
+        columns, tokens, 1, "gather_heads",
+    )
+    s = lax.dynamic_slice_in_dim(s, lax.axis_index("head") * heads, heads, axis=1)
     s = s.astype(F32)
     rows = q.shape[0]
     spans = rows // SPAN
@@ -308,10 +468,16 @@
         name="grad_part",
     )(q, k, v, g, o, s, *saved, state_in, grad_in)
 
-    def returned(array):
-        return lax.all_to_all(array, "head", split_axis=0, concat_axis=1, tiled=True)
-
-    return (returned(dq), returned(dk), returned(dv), returned(ds.astype(BF16)), returned(dg))
+    def own_columns(index, ref, peer):
+        return ref.at[peer] if index == 4 else columns(index, ref, peer)
+
+    dq, dk, dv, dg, ds = exchange(
+        (dq, dk, dv, dg, ds.astype(BF16)),
+        [jax.ShapeDtypeStruct((share, n * local_width), BF16)] * 4
+        + [jax.ShapeDtypeStruct((n, share, heads), BF16)],
+        tokens, own_columns, 2, "return_heads",
+    )
+    return dq, dk, dv, jnp.transpose(ds, (1, 0, 2)).reshape(share, heads_all), dg
 
 
 def solution(mesh):

time: 419 us -> 217 us (0.52)
  the two profiles are of different devices: /device:TPU:2 before, /device:TPU:0 now
where the time goes in v2:
time: 217 us; the launch traced here: 216 us
  Pallas kernels  206 us (95%)
  local copies, waits for them, and re-layouts  9.85 us (5%)
    pallas_call x2, Pallas kernels, exchange(): pl.pallas_call(functools.partial(exchange_kernel, n, count, source, targe...  114 us
    pallas_call x1, Pallas kernels, per_device(): pl.pallas_call(functools.partial(local_kernel, SPAN), grid=(heads,), in_s...  41.8 us
    pallas_call x1, Pallas kernels, per_device(): pl.pallas_call(functools.partial(grad_kernel, SPAN), grid=(heads,), in_sp...  26 us
    pallas_call x1, Pallas kernels, relay(): pl.pallas_call(functools.partial(relay_kernel, lax.axis_size('ctx')), in_...  23.6 us
    unnamed x15, local copies, waits for them, and re-layouts  9.16 us

profile of v2, /device:TPU:0, one launch (start us, length us, event | category | flops | bytes accessed | tf_op | source)
XLA Modules:
  0.0 216.5 jit_solution(10691224760443402271)
XLA Ops:
  0.6 0.8 copy.12.refs_5_
  1.4 0.0 copy-start
  1.4 1.0 copy-done
  2.5 0.0 copy-start.1
  2.5 1.0 copy-done.1
  3.5 0.0 copy-start.2
  3.5 1.0 copy-done.2
  4.6 0.0 copy-start.3
  4.6 1.0 copy-done.3
  5.6 0.0 copy-start.4
  5.6 1.0 copy-done.4
  6.6 63.8 %gather_heads.1 = (bf16[256,1024]{1,0:T(8,128)(2,1)S(1)}, bf16[256,1024]{1,0:T(8,128)(2,1)S(1)}, bf16[256,1024]{1,0:T(8,128)(2,1)S(1)}, bf16[256,1024]{1,0:T(8,1...) custom-call(bf16[64,4096]{1,0:T(8,128)(2,1)S(1)} %copy-done, bf16[64,4096]{1,0:T(8,128)(2,1)S(1)} %copy-done.1, ...), custom_call_target="tpu_custom_call" | custom-call | tf_op jit(solution)/shard_map/gather_heads/pallas_call | solution.py:394
  70.5 0.1 dynamic-slice_convert_fusion.b_ref
  70.6 41.8 %local_part.1 = (f32[8,256,128]{2,1,0:T(8,128)S(1)}, f32[8,256,128]{2,1,0:T(8,128)S(1)}, f32[8,256,256]{2,1,0:T(8,128)S(1)}, f32[8,256,256]{2,1,0:T(8,128)S(1)},...) custom-call(bf16[256,1024]{1,0:T(8,128)(2,1)S(1)} %get-tuple-element, ...), custom_call_target="tpu_custom_call" | custom-call | tf_op jit(solution)/shard_map/local_part/pallas_call | solution.py:449
  112.4 23.6 %relay.1 = (f32[8,128,128]{2,1,0:T(8,128)S(1)}, f32[8,128,128]{2,1,0:T(8,128)S(1)}) custom-call(f32[8,128,128]{2,1,0:T(8,128)S(1)} %get-tuple-element.48.trans_ref, f32[8,128,128]{2,1,0:T(8,128)S(1)} %get-tuple-element.49.end_ref, f32[8,128,128]{2,1,0:T(8,128)S(1)} %get-tuple-element.50.inject_ref), custom_call_target="tpu_custom_call" | custom-call | tf_op jit(solution)/shard_map/relay/pallas_call | solution.py:348
  136.0 26.0 %grad_part.1 = (bf16[256,1024]{1,0:T(8,128)(2,1)S(1)}, bf16[256,1024]{1,0:T(8,128)(2,1)S(1)}, bf16[256,1024]{1,0:T(8,128)(2,1)S(1)}, bf16[256,1024]{1,0:T(8,128)(2,1)S(1)}, f32[256,8]{1,0:T(8,128)S(1)}) custom-call(bf16[256,1024]{1,0:T(8,128)(2,1)S(1)} %get-tuple-element.34.q_ref, bf16[256,1024]{1,0:T(8,128)(2,1)S(1)} %get-tuple-element.35.k_ref, ...), custom_call_target="tpu_custom_call" | custom-call | tf_op jit(solution)/shard_map/grad_part/pallas_call | solution.py:461
  162.0 50.6 %return_heads.1 = (bf16[64,4096]{1,0:T(8,128)(2,1)S(1)}, bf16[64,4096]{1,0:T(8,128)(2,1)S(1)}, bf16[64,4096]{1,0:T(8,128)(2,1)S(1)}, bf16[64,4096]{1,0:T(8,128)(2,1)S(1)}, bf16[4,64,8]{2,1,0:T(8,128)(2,1)S(1)}) custom-call(bf16[256,1024]{1,0:T(8,128)(2,1)S(1)} %get-tuple-element.53.refs_0_, bf16[256,1024]{1,0:T(8,128)(2,1)S(1)} %get-tuple-element.54.refs_1_, ...), custom_call_target="tpu_custom_call" | custom-call | tf_op jit(solution)/shard_map/return_heads/pallas_call | solution.py:394
  212.6 0.7 copy.13
  213.3 0.8 copy.18
  214.1 0.8 copy.19
  214.9 0.8 copy.20
  215.7 0.8 copy.21
  (1 shorter events, 0.0 us)
Async XLA Ops:
  1.4 1.0 copy-start
  2.5 1.0 copy-start.1
  3.5 1.0 copy-start.2
  4.6 1.0 copy-start.3
  5.6 1.0 copy-start.4

commit v3 on v2

--- a/solution.py
+++ b/solution.py
@@ -103,17 +103,98 @@
     return found
 
 
-def local_kernel(span, q_ref, k_ref, v_ref, g_ref, o_ref, b_ref, ev_ref, ek_ref, inv_ref, a_ref, sc_ref,
-                 tr_ref, bs_ref, gs_ref, end_ref, trans_ref, inject_ref):
+def gather_head(n, ins, held, table_ref, table_held, send, recv, own, t_send, t_recv, t_own):
+    me = lax.axis_index("head")
+    step_index = pl.program_id(0)
+    heads, rows, width = held.shape[1:]
+    share = rows // n
+    mine = pl.ds(pl.multiple_of(me * share, share), share)
+
+    def source(index, h, peer):
+        return ins[index].at[:, pl.ds(pl.multiple_of((peer * heads + h) * width, width), width)]
+
+    def local(index, h):
+        return pltpu.make_async_copy(source(index, h, me), held.at[index, h, mine], own.at[h, index])
+
+    def remote(index, h, step):
+        peer = lax.rem(me + step, n)
+        return pltpu.make_async_remote_copy(
+            src_ref=source(index, h, peer), dst_ref=held.at[index, h, mine], send_sem=send.at[h, index, step],
+            recv_sem=recv.at[h, index, step], device_id={"head": peer}, device_id_type=MESH,
+        )
+
+    def table_local():
+        return pltpu.make_async_copy(table_ref, table_held.at[mine], t_own)
+
+    def table_remote(step):
+        return pltpu.make_async_remote_copy(
+            src_ref=table_ref, dst_ref=table_held.at[mine], send_sem=t_send.at[step],
+            recv_sem=t_recv.at[step], device_id={"head": lax.rem(me + step, n)}, device_id_type=MESH,
+        )
+
+    @pl.when(step_index == 0)
+    def _():
+        barrier = pltpu.get_barrier_semaphore()
+        for step in range(1, n):
+            pl.semaphore_signal(
+                barrier, inc=1, device_id={"head": lax.rem(me + step, n)}, device_id_type=MESH
+            )
+        table_local().start()
+
+        def start_local(h, carry):
+            for index in range(len(ins)):
+                local(index, h).start()
+            return carry
+
+        lax.fori_loop(0, heads, start_local, 0)
+        pl.semaphore_wait(barrier, n - 1)
+        for step in range(1, n):
+            table_remote(step).start()
+
+        def start_remote(h, carry):
+            for index in range(len(ins)):
+                for step in range(1, n):
+                    remote(index, h, step).start()
+            return carry
+
+        lax.fori_loop(0, heads, start_remote, 0)
+        table_local().wait()
+        for step in range(1, n):
+            table_remote(step).wait_recv()
+
+    for index in range(len(ins)):
+        local(index, step_index).wait()
+        for step in range(1, n):
+            remote(index, step_index, step).wait_recv()
+
+    @pl.when(step_index == heads - 1)
+    def _():
+        for step in range(1, n):
+            table_remote(step).wait_send()
+
+        def finish(h, carry):
+            for index in range(len(ins)):
+                for step in range(1, n):
+                    remote(index, h, step).wait_send()
+            return carry
+
+        lax.fori_loop(0, heads, finish, 0)
+
+
+def local_kernel(n, span, q_ref, k_ref, v_ref, g_ref, o_ref, b_ref, ev_ref, ek_ref, inv_ref, a_ref, sc_ref,
+                 tr_ref, bs_ref, gs_ref, end_ref, trans_ref, inject_ref, q_out, k_out, g_out, o_out, beta_out,
+                 held, table_held, send, recv, own, t_send, t_recv, t_own):
     head_index = pl.program_id(0)
-    rows, width = q_ref.shape
+    gather_head(n, (k_ref, g_ref, q_ref, v_ref, o_ref), held, b_ref, table_held, send, recv, own, t_send, t_recv, t_own)
+    heads, rows, width = held.shape[1:]
     spans = rows // span
-    q = q_ref[...].astype(F32)
-    k = k_ref[...].astype(F32)
-    v = v_ref[...]
-    o = o_ref[...]
-    beta = column_of(b_ref[...], head_index)
-    rise, fall, head, tail, fade = gates(g_ref[...], span)
+    k_raw, g, q_raw, v, o = (held[index, head_index] for index in range(5))
+    k_out[0], g_out[0], q_out[0], o_out[0] = k_raw, g, q_raw, o
+    q = q_raw.astype(F32)
+    k = k_raw.astype(F32)
+    beta = column_of(table_held[...].astype(F32), lax.axis_index("head") * heads + head_index)
+    beta_out[0] = beta
+    rise, fall, head, tail, fade = gates(g, span)
     q_unit = q * norm_of(q) * width ** (-0.5)
     k_unit = k * norm_of(k)
     row, col = grids(rows)
@@ -163,16 +244,63 @@
     inject_ref[0] = grad
 
 
-def grad_kernel(span, q_ref, k_ref, v_ref, g_ref, o_ref, b_ref, ev_ref, ek_ref, inv_ref, a_ref, sc_ref,
-                tr_ref, bs_ref, gs_ref, state_ref, dstate_ref, dq_ref, dk_ref, dv_ref, dg_ref, db_ref):
+def grad_kernel(n, span, q_ref, k_ref, g_ref, o_ref, b_ref, ev_ref, ek_ref, inv_ref, a_ref, sc_ref,
+                tr_ref, bs_ref, gs_ref, state_ref, dstate_ref, dq_out, dk_out, dv_out, dg_out, db_out,
+                done, db_all, db_done, send, recv, own, t_send, t_recv, t_own):
     head_index = pl.program_id(0)
-    rows, width = q_ref.shape
+    me = lax.axis_index("head")
+    outs = (dv_out, dq_out, dk_out, dg_out)
+    heads, rows, width = done.shape[1:]
+    share = rows // n
     spans = rows // span
-    q = q_ref[...].astype(F32)
-    k = k_ref[...].astype(F32)
-    o = o_ref[...]
-    beta = column_of(b_ref[...], head_index)
-    rise, fall, head, tail, fade = gates(g_ref[...], span)
+
+    def part(peer):
+        return pl.ds(pl.multiple_of(peer * share, share), share)
+
+    def target(index, h):
+        return outs[index].at[:, pl.ds(pl.multiple_of((me * heads + h) * width, width), width)]
+
+    def local(index, h):
+        return pltpu.make_async_copy(done.at[index, h, part(me)], target(index, h), own.at[h, index])
+
+    def remote(index, h, step):
+        peer = lax.rem(me + step, n)
+        return pltpu.make_async_remote_copy(
+            src_ref=done.at[index, h, part(peer)], dst_ref=target(index, h), send_sem=send.at[h, index, step],
+            recv_sem=recv.at[h, index, step], device_id={"head": peer}, device_id_type=MESH,
+        )
+
+    def table_local():
+        return pltpu.make_async_copy(db_done.at[part(me)], db_out.at[me], t_own)
+
+    def table_remote(step):
+        peer = lax.rem(me + step, n)
+        return pltpu.make_async_remote_copy(
+            src_ref=db_done.at[part(peer)], dst_ref=db_out.at[me], send_sem=t_send.at[step],
+            recv_sem=t_recv.at[step], device_id={"head": peer}, device_id_type=MESH,
+        )
+
+    def emit(index, value):
+        done[index, head_index] = value.astype(BF16)
+        local(index, head_index).start()
+        for step in range(1, n):
+            remote(index, head_index, step).start()
+
+    @pl.when(head_index == 0)
+    def _():
+        barrier = pltpu.get_barrier_semaphore()
+        for step in range(1, n):
+            pl.semaphore_signal(
+                barrier, inc=1, device_id={"head": lax.rem(me + step, n)}, device_id_type=MESH
+            )
+        db_all[...] = jnp.zeros_like(db_all)
+        pl.semaphore_wait(barrier, n - 1)
+
+    q = q_ref[0].astype(F32)
+    k = k_ref[0].astype(F32)
+    o = o_ref[0]
+    beta = b_ref[0]
+    rise, fall, head, tail, fade = gates(g_ref[0], span)
     q_norm = norm_of(q)
     k_norm = norm_of(k)
     q_unit = q * q_norm * width ** (-0.5)
@@ -199,11 +327,11 @@
     d_update = dot3(split(sc_ref[0].T), o) + each(lambda i, at: dot3(rows_of(k_tail_s, at, span), grads_s[i]))
     d_value = dot3(split(inv_ref[0].T), split(d_update * beta))
     d_value_s = split(d_value)
-    dv_ref[...] = d_value.astype(BF16)
+    emit(0, d_value)
     residue = d_update - dot3(split(a_ref[0].T), d_value_s)
     d_beta = jnp.sum(error * residue, axis=1, keepdims=True)
-    lane = lax.broadcasted_iota(jnp.int32, b_ref.shape, 1)
-    db_ref[...] = jnp.where(lane == head_index, d_beta, db_ref[...])
+    lane = lax.broadcasted_iota(jnp.int32, db_all.shape, 1)
+    db_all[...] = jnp.where(lane == head_index, d_beta, db_all[...])
     dq_head = each(lambda i, at: dot3(o[at : at + span], states_s[i], NT))
     dk_head = -each(lambda i, at: dot3(rows_of(d_value_s, at, span), states_s[i], NT))
     dk_tail = each(lambda i, at: dot3(rows_of(update_s, at, span), grads_s[i], NT))
@@ -229,13 +357,32 @@
     last = jnp.concatenate([x.reshape(1, 1, width) for x in last], axis=0)
     sum_mask = jnp.where(inside & (col >= row), 1.0, 0.0).astype(BF16)
     d_decay = dot3(sum_mask, split(d_gamma)) + per_span(tail_sum + last, span, d_gamma)
-    dg_ref[...] = d_decay.astype(BF16)
     scale = width ** (-0.5)
     dq = (dq_unit - q * (q_norm * q_norm * jnp.sum(q * dq_unit, axis=1, keepdims=True))) * (q_norm * scale)
-    dq_ref[...] = dq.astype(BF16)
+    emit(1, dq)
     dk_unit = up + down
     dk = (dk_unit - k * (k_norm * k_norm * jnp.sum(k * dk_unit, axis=1, keepdims=True))) * k_norm
-    dk_ref[...] = dk.astype(BF16)
+    emit(2, dk)
+    emit(3, d_decay)
+
+    @pl.when(head_index == heads - 1)
+    def _():
+        db_done[...] = db_all[...].astype(BF16)
+        table_local().start()
+        for step in range(1, n):
+            table_remote(step).start()
+
+        def finish(h, carry):
+            for index in range(len(outs)):
+                local(index, h).wait()
+                for step in range(1, n):
+                    remote(index, h, step).wait()
+            return carry
+
+        lax.fori_loop(0, heads, finish, 0)
+        table_local().wait()
+        for step in range(1, n):
+            table_remote(step).wait()
 
 
 def relay_kernel(n, trans_ref, end_ref, inject_ref, state_ref, grad_ref, move_ref, turn_ref, in_f, in_b, out_f, out_b,
@@ -358,125 +505,66 @@
     )(trans, ends, inject)
 
 
-def exchange_kernel(n, count, source, target, *refs):
-    ins, outs = refs[:count], refs[count : 2 * count]
-    send, recv, own = refs[2 * count :]
-    me = lax.axis_index("head")
-    barrier = pltpu.get_barrier_semaphore()
-    for step in range(1, n):
-        pl.semaphore_signal(
-            barrier, inc=1, device_id={"head": lax.rem(me + step, n)}, device_id_type=MESH
-        )
-    local = [
-        pltpu.make_async_copy(source(i, a, me), target(i, b, me), own.at[i])
-        for i, (a, b) in enumerate(zip(ins, outs))
-    ]
-    for copy in local:
-        copy.start()
-    pl.semaphore_wait(barrier, n - 1)
-    copies = []
-    for i, (a, b) in enumerate(zip(ins, outs)):
-        for step in range(1, n):
-            peer = lax.rem(me + step, n)
-            copy = pltpu.make_async_remote_copy(
-                src_ref=source(i, a, peer), dst_ref=target(i, b, me), send_sem=send.at[i, step],
-                recv_sem=recv.at[i, step], device_id={"head": peer}, device_id_type=MESH,
-            )
-            copy.start()
-            copies.append(copy)
-    for copy in local + copies:
-        copy.wait()
-
-
-def exchange(arrays, types, source, target, identity, name):
-    count, n = len(arrays), lax.axis_size("head")
-    whole = pl.BlockSpec(memory_space=pltpu.VMEM)
-    return pl.pallas_call(
-        functools.partial(exchange_kernel, n, count, source, target),
-        in_specs=[whole] * count,
-        out_specs=[whole] * count,
-        out_shape=types,
-        scratch_shapes=[pltpu.SemaphoreType.DMA((count, n))] * 2 + [pltpu.SemaphoreType.DMA((count,))],
-        compiler_params=pltpu.CompilerParams(
-            collective_id=identity, has_side_effects=True, vmem_limit_bytes=40 * 1024 * 1024
-        ),
-        name=name,
-    )(*arrays)
-
-
 def per_device(queries, key_in, values_in, strength, log_decay, d_out):
     heads_all = strength.shape[1]
-    heads = heads_all // lax.axis_size("head")
+    n = lax.axis_size("head")
+    heads = heads_all // n
     width = queries.shape[1] // heads_all
-
-    n = lax.axis_size("head")
     share = queries.shape[0]
-    local_width = heads * width
-
-    def columns(index, ref, peer):
-        if index == 5:
-            return ref
-        return ref.at[:, pl.ds(pl.multiple_of(peer * local_width, local_width), local_width)]
-
-    def tokens(index, ref, peer):
-        return ref.at[pl.ds(pl.multiple_of(peer * share, share), share)]
-
-    k, g, q, v, o, s = exchange(
-        (key_in, log_decay, queries, values_in, d_out, strength),
-        [jax.ShapeDtypeStruct((n * share, local_width), BF16)] * 5
-        + [jax.ShapeDtypeStruct((n * share, heads_all), BF16)],
-        columns, tokens, 1, "gather_heads",
-    )
-    s = lax.dynamic_slice_in_dim(s, lax.axis_index("head") * heads, heads, axis=1)
-    s = s.astype(F32)
-    rows = q.shape[0]
+    rows = n * share
     spans = rows // SPAN
-    token = pl.BlockSpec((rows, width), lambda h: (0, h))
-    table = pl.BlockSpec((rows, heads), lambda h: (0, 0))
+    outside = pl.BlockSpec(memory_space=pl.ANY)
     narrow = pl.BlockSpec((1, rows, width), lambda h: (h, 0, 0))
     square = pl.BlockSpec((1, rows, rows), lambda h: (h, 0, 0))
     state = pl.BlockSpec((1, width, width), lambda h: (h, 0, 0))
     state_list = pl.BlockSpec((1, spans, width, width), lambda h: (h, 0, 0, 0))
-    inputs = [token] * 5 + [table]
+    column = pl.BlockSpec((1, rows, 1), lambda h: (h, 0, 0))
     narrow_t = jax.ShapeDtypeStruct((heads, rows, width), F32)
+    token_t = jax.ShapeDtypeStruct((heads, rows, width), BF16)
     square_t = jax.ShapeDtypeStruct((heads, rows, rows), F32)
     state_t = jax.ShapeDtypeStruct((heads, width, width), F32)
     state_list_t = jax.ShapeDtypeStruct((heads, spans, width, width), F32)
-    token_t = jax.ShapeDtypeStruct((rows, heads * width), BF16)
-    params = pltpu.CompilerParams(dimension_semantics=("arbitrary",), vmem_limit_bytes=40 * 1024 * 1024)
+    column_t = jax.ShapeDtypeStruct((heads, rows, 1), F32)
+    dma = pltpu.SemaphoreType.DMA
+
+    def params(identity):
+        return pltpu.CompilerParams(
+            dimension_semantics=("arbitrary",), vmem_limit_bytes=48 * 1024 * 1024,
+            collective_id=identity, has_side_effects=True,
+        )
+
+    def semaphores(count):
+        return [dma((heads, count, n))] * 2 + [dma((heads, count))] + [dma((n,))] * 2 + [dma(())]
+
     saved_specs = [narrow] * 2 + [square] * 3 + [state_list] * 3
     saved_types = [narrow_t] * 2 + [square_t] * 3 + [state_list_t] * 3
     results = pl.pallas_call(
-        functools.partial(local_kernel, SPAN),
+        functools.partial(local_kernel, n, SPAN),
         grid=(heads,),
-        in_specs=inputs,
-        out_specs=saved_specs + [state] * 3,
-        out_shape=saved_types + [state_t] * 3,
-        compiler_params=params,
+        in_specs=[outside] * 6,
+        out_specs=saved_specs + [state] * 3 + [narrow] * 4 + [column],
+        out_shape=saved_types + [state_t] * 3 + [token_t] * 4 + [column_t],
+        scratch_shapes=[pltpu.VMEM((5, heads, rows, width), BF16), pltpu.VMEM((rows, heads_all), BF16)] + semaphores(5),
+        compiler_params=params(1),
         name="local_part",
-    )(q, k, v, g, o, s)
+    )(queries, key_in, values_in, log_decay, d_out, strength)
     saved = results[:8]
-    ends, trans, inject = results[8:]
+    ends, trans, inject = results[8:11]
+    moved = results[11:]
     state_in, grad_in = relay(trans, ends, inject)
+    full_t = jax.ShapeDtypeStruct(queries.shape, BF16)
     dq, dk, dv, dg, ds = pl.pallas_call(
-        functools.partial(grad_kernel, SPAN),
+        functools.partial(grad_kernel, n, SPAN),
         grid=(heads,),
-        in_specs=inputs + saved_specs + [state] * 2,
-        out_specs=[token] * 4 + [table],
-        out_shape=[token_t] * 4 + [jax.ShapeDtypeStruct((rows, heads), F32)],
-        compiler_params=params,
+        in_specs=[narrow] * 4 + [column] + saved_specs + [state] * 2,
+        out_specs=[outside] * 5,
+        out_shape=[full_t] * 4 + [jax.ShapeDtypeStruct((n, share, heads), BF16)],
+        scratch_shapes=[
+            pltpu.VMEM((4, heads, rows, width), BF16), pltpu.VMEM((rows, heads), F32), pltpu.VMEM((rows, heads), BF16)
+        ] + semaphores(4),
+        compiler_params=params(2),
         name="grad_part",
-    )(q, k, v, g, o, s, *saved, state_in, grad_in)
-
-    def own_columns(index, ref, peer):
-        return ref.at[peer] if index == 4 else columns(index, ref, peer)
-
-    dq, dk, dv, dg, ds = exchange(
-        (dq, dk, dv, dg, ds.astype(BF16)),
-        [jax.ShapeDtypeStruct((share, n * local_width), BF16)] * 4
-        + [jax.ShapeDtypeStruct((n, share, heads), BF16)],
-        tokens, own_columns, 2, "return_heads",
-    )
+    )(*moved, *saved, state_in, grad_in)
     return dq, dk, dv, jnp.transpose(ds, (1, 0, 2)).reshape(share, heads_all), dg
 
 

time: 217 us -> 170 us (0.78)
  Pallas kernels: 206 us -> 160 us
    pallas_call x4 -> x2, Pallas kernels: 182 us -> 136 us  [the longest x1 79.6 us: per_device(): pl.pallas_call(functools.partial(local_kernel, n, SPAN), grid=(heads,), i...]
    unnamed x15 -> x13, local copies, waits for them, and re-layouts: 9.16 us -> 8.12 us
where the time goes in v3:
time: 170 us; the launch traced here: 169 us
  Pallas kernels  160 us (94%)
  local copies, waits for them, and re-layouts  8.8 us (5%)
    pallas_call x1, Pallas kernels, per_device(): pl.pallas_call(functools.partial(local_kernel, n, SPAN), grid=(heads,), i...  79.6 us
    pallas_call x1, Pallas kernels, per_device(): pl.pallas_call(functools.partial(grad_kernel, n, SPAN), grid=(heads,), in...  56.6 us
    pallas_call x1, Pallas kernels, relay(): pl.pallas_call(functools.partial(relay_kernel, lax.axis_size('ctx')), in_...  23.6 us
    unnamed x13, local copies, waits for them, and re-layouts  8.12 us

profile of v3, /device:TPU:0, one launch (start us, length us, event | category | flops | bytes accessed | tf_op | source)
XLA Modules:
  0.0 169.2 jit_solution(4468864158314858367)
XLA Ops:
  0.6 0.8 copy.12.b_ref
  1.4 0.0 copy-start
  1.4 1.0 copy-done
  2.5 0.0 copy-start.1
  2.5 1.0 copy-done.1
  3.5 0.0 copy-start.2
  3.5 1.0 copy-done.2
  4.6 0.0 copy-start.3
  4.6 1.0 copy-done.3
  5.6 79.6 %local_part.1 = (f32[8,256,128]{2,1,0:T(8,128)}, f32[8,256,128]{2,1,0:T(8,128)}, f32[8,256,256]{2,1,0:T(8,128)}, f32[8,256,256]{2,1,0:T(8,128)}, f32[8,256,256]{...) custom-call(bf16[64,4096]{1,0:T(8,128)(2,1)S(1)} %copy-done, ...), custom_call_target="tpu_custom_call" | custom-call | tf_op jit(solution)/shard_map/local_part/pallas_call | solution.py:541
  85.2 23.6 %relay.1 = (f32[8,128,128]{2,1,0:T(8,128)S(1)}, f32[8,128,128]{2,1,0:T(8,128)S(1)}) custom-call(f32[8,128,128]{2,1,0:T(8,128)S(1)} %get-tuple-element.41.trans_ref, f32[8,128,128]{2,1,0:T(8,128)S(1)} %get-tuple-element.42.end_ref, f32[8,128,128]{2,1,0:T(8,128)S(1)} %get-tuple-element.43.inject_ref), custom_call_target="tpu_custom_call" | custom-call | tf_op jit(solution)/shard_map/relay/pallas_call | solution.py:495
  108.8 56.6 %grad_part.1 = (bf16[64,4096]{1,0:T(8,128)(2,1)S(1)}, bf16[64,4096]{1,0:T(8,128)(2,1)S(1)}, bf16[64,4096]{1,0:T(8,128)(2,1)S(1)}, bf16[64,4096]{1,0:T(8,128)(2,1)S(1)}, bf16[4,64,8]{2,1,0:T(8,128)(2,1)S(1)}) custom-call(bf16[8,256,128]{2,1,0:T(8,128)(2,1)S(1)} %get-tuple-element.28.q_ref, bf16[8,256,128]{2,1,0:T(8,128)(2,1)S(1)} %get-tuple-element.29.k_ref, ...), custom_call_target="tpu_custom_call" | custom-call | tf_op jit(solution)/shard_map/grad_part/pallas_call | solution.py:556
  165.4 0.7 copy.13
  166.1 0.8 copy.18
  166.9 0.8 copy.19
  167.7 0.8 copy.20
  168.4 0.8 copy.21
Async XLA Ops:
  1.4 1.0 copy-start
  2.5 1.0 copy-start.1
  3.5 1.0 copy-start.2
  4.6 1.0 copy-start.3

commit v4 on v1

v4 whole, which is shorter than its diff:
```python
import functools

import jax
import jax.numpy as jnp
from jax import lax
from jax.experimental import pallas as pl
from jax.experimental.pallas import tpu as pltpu
from jax.sharding import PartitionSpec as P

SPAN = 64
BASE = 8
EPS = 1e-06
F32 = jnp.float32
BF16 = jnp.bfloat16
MESH = pl.DeviceIdType.MESH

NN = (((1,), (0,)), ((), ()))
NT = (((1,), (1,)), ((), ()))


def split(x):
    high = x.astype(BF16)
    return high, (x - high.astype(F32)).astype(BF16)


def mul(a, b, dims=NN):
    return lax.dot_general(a, b, dims, preferred_element_type=F32)


def dot3(a, b, dims=NN):
    if not isinstance(a, tuple):
        return mul(a, b[0], dims) + mul(a, b[1], dims)
    if not isinstance(b, tuple):
        return mul(a[0], b, dims) + mul(a[1], b, dims)
    return mul(a[0], b[0], dims) + (mul(a[0], b[1], dims) + mul(a[1], b[0], dims))


def rows_of(pair, start, size):
    if not isinstance(pair, tuple):
        return pair[start : start + size]
    return tuple(part[start : start + size] for part in pair)


def both(a, b, axis):
    return tuple(jnp.concatenate([x, y], axis=axis) for x, y in zip(a, b))


def grids(size):
    return (
        lax.broadcasted_iota(jnp.int32, (size, size), 0),
        lax.broadcasted_iota(jnp.int32, (size, size), 1),
    )


def per_span(row_values, span, like):
    rows, width = like.shape
    return jnp.broadcast_to(row_values, (rows // span, span, width)).reshape(rows, width)


def gates(g, span):
    rows, width = g.shape
    row, col = grids(rows)
    sum_mask = jnp.where((row // span == col // span) & (col <= row), 1.0, 0.0).astype(BF16)
    gamma = mul(sum_mask, g)
    spans = gamma.reshape(rows // span, span, width)
    middle = spans[:, span // 2 - 1 : span // 2]
    end = spans[:, span - 1 : span]
    centred = gamma - per_span(middle, span, gamma)
    rise = jnp.exp(centred)
    fall = jnp.exp(-centred)
    head = rise * per_span(jnp.exp(middle), span, gamma)
    tail = fall * per_span(jnp.exp(end - middle), span, gamma)
    fade = jnp.exp(end).reshape(rows // span, width)
    return rise, fall, head, tail, fade


def column_of(table, index):
    lane = lax.broadcasted_iota(jnp.int32, table.shape, 1)
    return jnp.sum(jnp.where(lane == index, table, 0.0), axis=1, keepdims=True)


def norm_of(x):
    return lax.rsqrt(jnp.sum(x * x, axis=1, keepdims=True) + EPS)


def inverse(system, row, col):
    same = row // BASE == col // BASE
    near = jnp.where(same, system, 0.0)
    near_s = split(near)
    square = dot3(near_s, near_s)
    square_s = split(square)
    found = jnp.where(row == col, 1.0, 0.0) - near
    fourth = dot3(square_s, square_s)
    found = found + dot3(split(found), square_s)
    found = found + dot3(split(found), split(fourth))
    block = BASE
    while block < SPAN:
        wide = row // (2 * block) == col // (2 * block)
        off = jnp.where(wide & (row // block != col // block), system, 0.0)
        found_s = split(found)
        found = found - dot3(found_s, split(dot3(split(off), found_s)))
        block *= 2
    return found


def gatherer(n, ins, held, table_ref, table_held, send, recv, own, t_send, t_recv, t_own):
    me = lax.axis_index("head")
    heads, rows, width = held.shape[1:]
    share = rows // n
    mine = pl.ds(pl.multiple_of(me * share, share), share)

    def source(index, h, peer):
        return ins[index].at[:, pl.ds(pl.multiple_of((peer * heads + h) * width, width), width)]

    def local(index, h):
        return pltpu.make_async_copy(source(index, h, me), held.at[index, h, mine], own.at[h, index])

    def remote(index, h, step):
        peer = lax.rem(me + step, n)
        return pltpu.make_async_remote_copy(
            src_ref=source(index, h, peer), dst_ref=held.at[index, h, mine], send_sem=send.at[h, index, step],
            recv_sem=recv.at[h, index, step], device_id={"head": peer}, device_id_type=MESH,
        )

    def table_local():
        return pltpu.make_async_copy(table_ref, table_held.at[mine], t_own)

    def table_remote(step):
        return pltpu.make_async_remote_copy(
            src_ref=table_ref, dst_ref=table_held.at[mine], send_sem=t_send.at[step],
            recv_sem=t_recv.at[step], device_id={"head": lax.rem(me + step, n)}, device_id_type=MESH,
        )

    def start():
        for step in range(1, n):
            table_remote(step).start()

        def start_remote(h, carry):
            for index in range(len(ins)):
                for step in range(1, n):
                    remote(index, h, step).start()
            return carry

        lax.fori_loop(0, heads, start_remote, 0)
        table_local().start()

        def start_local(h, carry):
            for index in range(len(ins)):
                local(index, h).start()
            return carry

        lax.fori_loop(0, heads, start_local, 0)
        table_local().wait()
        for step in range(1, n):
            table_remote(step).wait_recv()

    def arrive(h):
        for index in range(len(ins)):
            local(index, h).wait()
            for step in range(1, n):
                remote(index, h, step).wait_recv()

    def finish():
        for step in range(1, n):
            table_remote(step).wait_send()

        def finish_head(h, carry):
            for index in range(len(ins)):
                for step in range(1, n):
                    remote(index, h, step).wait_send()
            return carry

        lax.fori_loop(0, heads, finish_head, 0)

    return start, arrive, finish


def local_part(h, span, held, table_held, saved, total_ref):
    ev_ref, ek_ref, inv_ref, a_ref, sc_ref, tr_ref, bs_ref, gs_ref = saved
    heads, rows, width = held.shape[1:]
    spans = rows // span
    k, g, q, v, o = (held[index, h] for index in range(5))
    q = q.astype(F32)
    k = k.astype(F32)
    beta = column_of(table_held[...].astype(F32), lax.axis_index("head") * heads + h)
    rise, fall, head, tail, fade = gates(g, span)
    q_unit = q * norm_of(q) * width ** (-0.5)
    k_unit = k * norm_of(k)
    row, col = grids(rows)
    inside = row // span == col // span
    k_fall_s = split(k_unit * fall)
    inner = jnp.where(inside & (col < row), dot3(split(k_unit * rise), k_fall_s, NT), 0.0)
    scores = jnp.where(inside & (col <= row), dot3(split(q_unit * rise), k_fall_s, NT), 0.0)
    a_ref[h] = inner
    sc_ref[h] = scores
    beta_row = jnp.sum(jnp.where(row == col, beta, 0.0), axis=0, keepdims=True)
    found = inverse(inner * beta_row, row, col)
    inv_ref[h] = found
    found_s = split(found)
    e_value = dot3(found_s, v)
    e_key = dot3(found_s, split(k_unit * head))
    ev_ref[h] = e_value
    ek_ref[h] = e_key
    w_key_s = split(e_key * beta)
    w_value_s = split(e_value * beta)
    reach = q_unit * head - dot3(split(scores), w_key_s)
    k_tail = k_unit * tail
    small_row, small_col = grids(width)
    diagonal = small_row == small_col
    moves, adds, backs = [], [], []
    for index in range(spans):
        at = index * span
        tail_t = split(k_tail[at : at + span].T)
        move = jnp.where(diagonal, fade[index : index + 1], 0.0) - dot3(tail_t, rows_of(w_key_s, at, span))
        add = dot3(tail_t, rows_of(w_value_s, at, span))
        back = dot3(split(reach[at : at + span].T), o[at : at + span])
        tr_ref[h, index] = move
        bs_ref[h, index] = add
        gs_ref[h, index] = back
        moves.append(move)
        adds.append(add)
        backs.append(back)
    trans, ends = moves[0], adds[0]
    grad = backs[spans - 1]
    for index in range(1, spans):
        move_s = split(moves[index])
        trans = dot3(move_s, split(trans))
        ends = dot3(move_s, split(ends)) + adds[index]
        mirror = spans - 1 - index
        grad = dot3(split(moves[mirror].T), split(grad)) + backs[mirror]
    total_ref[0, h, 0], total_ref[0, h, 1], total_ref[0, h, 2] = trans, ends, grad


def returner(n, done, db_done, outs, db_out, send, recv, own, t_send, t_recv, t_own):
    me = lax.axis_index("head")
    heads, rows, width = done.shape[1:]
    share = rows // n

    def part(peer):
        return pl.ds(pl.multiple_of(peer * share, share), share)

    def target(index, h):
        return outs[index].at[:, pl.ds(pl.multiple_of((me * heads + h) * width, width), width)]

    def local(index, h):
        return pltpu.make_async_copy(done.at[index, h, part(me)], target(index, h), own.at[h, index])

    def remote(index, h, step):
        peer = lax.rem(me + step, n)
        return pltpu.make_async_remote_copy(
            src_ref=done.at[index, h, part(peer)], dst_ref=target(index, h), send_sem=send.at[h, index, step],
            recv_sem=recv.at[h, index, step], device_id={"head": peer}, device_id_type=MESH,
        )

    def table_local():
        return pltpu.make_async_copy(db_done.at[part(me)], db_out.at[me], t_own)

    def table_remote(step):
        peer = lax.rem(me + step, n)
        return pltpu.make_async_remote_copy(
            src_ref=db_done.at[part(peer)], dst_ref=db_out.at[me], send_sem=t_send.at[step],
            recv_sem=t_recv.at[step], device_id={"head": peer}, device_id_type=MESH,
        )

    def emit(index, h, value):
        done[index, h] = value.astype(BF16)
        local(index, h).start()
        for step in range(1, n):
            remote(index, h, step).start()

    def finish():
        table_local().start()
        for step in range(1, n):
            table_remote(step).start()

        def finish_head(h, carry):
            for index in range(len(outs)):
                local(index, h).wait()
                for step in range(1, n):
                    remote(index, h, step).wait()
            return carry

        lax.fori_loop(0, heads, finish_head, 0)
        table_local().wait()
        for step in range(1, n):
            table_remote(step).wait()

    return emit, finish


def grad_part(h, span, held, table_held, saved, state_ref, dstate_ref, db_all, emit_head):
    ev_ref, ek_ref, inv_ref, a_ref, sc_ref, tr_ref, bs_ref, gs_ref = saved
    heads, rows, width = held.shape[1:]
    spans = rows // span
    k, g, q, _, o = (held[index, h] for index in range(5))
    q = q.astype(F32)
    k = k.astype(F32)
    beta = column_of(table_held[...].astype(F32), lax.axis_index("head") * heads + h)

    def emit(index, value):
        emit_head(index, h, value)

    rise, fall, head, tail, fade = gates(g, span)
    q_norm = norm_of(q)
    k_norm = norm_of(k)
    q_unit = q * q_norm * width ** (-0.5)
    k_unit = k * k_norm
    row, col = grids(rows)
    inside = row // span == col // span
    states = [state_ref[h]]
    grads = [dstate_ref[h]]
    for index in range(spans - 1):
        states.append(dot3(split(tr_ref[h, index]), split(states[-1])) + bs_ref[h, index])
        mirror = spans - 1 - index
        grads.insert(0, dot3(split(tr_ref[h, mirror].T), split(grads[0])) + gs_ref[h, mirror])
    states_s = [split(x) for x in states]
    grads_s = [split(x) for x in grads]

    def each(fn):
        return jnp.concatenate([fn(index, index * span) for index in range(spans)], axis=0)

    ek_s = split(ek_ref[h])
    k_tail = k_unit * tail
    k_tail_s = split(k_tail)
    error = ev_ref[h] - each(lambda i, at: dot3(rows_of(ek_s, at, span), states_s[i]))
    update_s = split(error * beta)
    d_update = dot3(split(sc_ref[h].T), o) + each(lambda i, at: dot3(rows_of(k_tail_s, at, span), grads_s[i]))
    d_value = dot3(split(inv_ref[h].T), split(d_update * beta))
    d_value_s = split(d_value)
    emit(0, d_value)
    residue = d_update - dot3(split(a_ref[h].T), d_value_s)
    d_beta = jnp.sum(error * residue, axis=1, keepdims=True)
    lane = lax.broadcasted_iota(jnp.int32, db_all.shape, 1)
    db_all[...] = jnp.where(lane == h, d_beta, db_all[...])
    dq_head = each(lambda i, at: dot3(o[at : at + span], states_s[i], NT))
    dk_head = -each(lambda i, at: dot3(rows_of(d_value_s, at, span), states_s[i], NT))
    dk_tail = each(lambda i, at: dot3(rows_of(update_s, at, span), grads_s[i], NT))
    d_scores = jnp.where(inside & (col <= row), dot3(o, update_s, NT), 0.0)
    d_inner = jnp.where(inside & (col < row), -dot3(d_value_s, update_s, NT), 0.0)
    k_fall_s = split(k_unit * fall)
    dq_rise = dot3(split(d_scores), k_fall_s)
    dk_rise = dot3(split(d_inner), k_fall_s)
    dk_fall = dot3(split(d_scores.T), split(q_unit * rise)) + dot3(split(d_inner.T), split(k_unit * rise))
    dq_unit = dq_rise * rise + dq_head * head
    up = dk_rise * rise + dk_head * head
    tail_part = dk_tail * tail
    down = dk_fall * fall + tail_part
    d_gamma = q_unit * dq_unit + k_unit * (up - down)
    tail_sum = jnp.sum((k_unit * tail_part).reshape(spans, span, width), axis=1, keepdims=True)
    small_row, small_col = grids(width)
    diagonal = small_row == small_col
    last = []
    for index in range(spans):
        d_fade = jnp.sum(states[index] * grads[index], axis=1, keepdims=True)
        d_fade = jnp.sum(jnp.where(diagonal, d_fade, 0.0), axis=0, keepdims=True)
        last.append(d_fade * fade[index : index + 1])
    last = jnp.concatenate([x.reshape(1, 1, width) for x in last], axis=0)
    sum_mask = jnp.where(inside & (col >= row), 1.0, 0.0).astype(BF16)
    d_decay = dot3(sum_mask, split(d_gamma)) + per_span(tail_sum + last, span, d_gamma)
    scale = width ** (-0.5)
    dq = (dq_unit - q * (q_norm * q_norm * jnp.sum(q * dq_unit, axis=1, keepdims=True))) * (q_norm * scale)
    emit(1, dq)
    dk_unit = up + down
    dk = (dk_unit - k * (k_norm * k_norm * jnp.sum(k * dk_unit, axis=1, keepdims=True))) * k_norm
    emit(2, dk)
    emit(3, d_decay)


def exchanger(total_ref, other_ref, send, recv):
    me = lax.axis_index("ctx")

    def partner(r):
        bit = 2**r
        return me + bit - 2 * bit * lax.rem(me // bit, 2)

    def swap(r, h):
        return pltpu.make_async_remote_copy(
            src_ref=total_ref.at[r, h], dst_ref=other_ref.at[r, h], send_sem=send.at[r, h],
            recv_sem=recv.at[r, h], device_id={"ctx": partner(r)}, device_id_type=MESH,
        )

    return partner, swap


def combine(r, rounds, h, total_ref, other_ref, lead_ref, trail_ref, state_ref, dstate_ref):
    upper = lax.rem(lax.axis_index("ctx") // 2**r, 2) == 1
    trans, ends, grad = (total_ref.at[r, h, index] for index in range(3))
    other, other_ends, other_grad = (other_ref.at[r, h, index] for index in range(3))
    more = r < rounds - 1

    @pl.when(upper)
    def _():
        other_s, ends_s = split(other[...]), split(other_ends[...])
        lead_s = split(lead_ref[h])
        state_ref[h] = state_ref[h] + dot3(lead_s, ends_s)
        if more:
            lead_ref[h] = dot3(lead_s, other_s)
            trans_s = split(trans[...])
            total_ref[r + 1, h, 0] = dot3(trans_s, other_s)
            total_ref[r + 1, h, 1] = dot3(trans_s, ends_s) + ends[...]
            total_ref[r + 1, h, 2] = other_grad[...] + dot3(split(other[...].T), split(grad[...]))

    @pl.when(jnp.logical_not(upper))
    def _():
        grad_s = split(other_grad[...])
        trail_s = split(trail_ref[h])
        dstate_ref[h] = dstate_ref[h] + dot3(trail_s, grad_s)
        if more:
            other_s = split(other[...])
            trail_ref[h] = dot3(trail_s, other_s, NT)
            trans_s = split(trans[...])
            total_ref[r + 1, h, 0] = dot3(other_s, trans_s)
            total_ref[r + 1, h, 1] = dot3(other_s, split(ends[...])) + other_ends[...]
            total_ref[r + 1, h, 2] = grad[...] + dot3(split(trans[...].T), grad_s)


def layer_kernel(n, rounds, span, q_ref, k_ref, v_ref, g_ref, o_ref, b_ref, dq_out, dk_out, dv_out, dg_out, db_out,
                 held, table_held, done, db_all, db_done, ev, ek, inv, a, sc, tr, bs, gs, total, other, lead, trail,
                 state, dstate, x_send, x_recv, *semaphores):
    t = pl.program_id(0)
    heads, width = held.shape[1], held.shape[3]
    saved = (ev, ek, inv, a, sc, tr, bs, gs)
    start, arrive, finish_in = gatherer(
        n, (k_ref, g_ref, q_ref, v_ref, o_ref), held, b_ref, table_held, *semaphores[:6]
    )
    emit, finish_out = returner(n, done, db_done, (dv_out, dq_out, dk_out, dg_out), db_out, *semaphores[6:])
    partner, swap = exchanger(total, other, x_send, x_recv)

    @pl.when(t == 0)
    def _():
        me = lax.axis_index("head")
        barrier = pltpu.get_barrier_semaphore()
        for step in range(1, n):
            pl.semaphore_signal(
                barrier, inc=1, device_id={"head": lax.rem(me + step, n)}, device_id_type=MESH
            )
        for r in range(rounds):
            pl.semaphore_signal(barrier, inc=1, device_id={"ctx": partner(r)}, device_id_type=MESH)
        db_all[...] = jnp.zeros_like(db_all)
        state[...] = jnp.zeros_like(state)
        dstate[...] = jnp.zeros_like(dstate)
        row, col = grids(width)
        unit = jnp.where(row == col, 1.0, 0.0)
        for h in range(heads):
            lead[h] = unit
            trail[h] = unit
        pl.semaphore_wait(barrier, n - 1 + rounds)
        start()

    def turn(r):
        h = t - 1 - r

        @pl.when((h >= 0) & (h < heads))
        def _():
            swap(r, h).wait_recv()
            combine(r, rounds, h, total, other, lead, trail, state, dstate)
            if r < rounds - 1:
                swap(r + 1, h).start()

    for r in range(rounds - 1, 0, -1):
        turn(r)

    if rounds == 1:
        turn(0)

    @pl.when(t >= rounds)
    def _():
        grad_part(t - rounds, span, held, table_held, saved, state, dstate, db_all, emit)

    if rounds > 1:
        turn(0)

    @pl.when(t < heads)
    def _():
        arrive(t)
        local_part(t, span, held, table_held, saved, total)
        swap(0, t).start()

    @pl.when(t == heads + rounds - 1)
    def _():
        db_done[...] = db_all[...].astype(BF16)
        finish_out()
        finish_in()

        def finish_swap(h, carry):
            for r in range(rounds):
                swap(r, h).wait_send()
            return carry

        lax.fori_loop(0, heads, finish_swap, 0)


def per_device(queries, key_in, values_in, strength, log_decay, d_out):
    heads_all = strength.shape[1]
    n = lax.axis_size("head")
    rounds = lax.axis_size("ctx").bit_length() - 1
    heads = heads_all // n
    width = queries.shape[1] // heads_all
    share = queries.shape[0]
    rows = n * share
    spans = rows // SPAN
    outside = pl.BlockSpec(memory_space=pl.ANY)
    full_t = jax.ShapeDtypeStruct(queries.shape, BF16)
    dma = pltpu.SemaphoreType.DMA
    vmem = pltpu.VMEM

    def semaphores(count):
        return [dma((heads, count, n))] * 2 + [dma((heads, count))] + [dma((n,))] * 2 + [dma(())]

    narrow = vmem((heads, rows, width), F32)
    square = vmem((heads, rows, rows), F32)
    state = vmem((heads, width, width), F32)
    state_list = vmem((heads, spans, width, width), F32)
    totals = vmem((rounds, heads, 3, width, width), F32)
    dq, dk, dv, dg, ds = pl.pallas_call(
        functools.partial(layer_kernel, n, rounds, SPAN),
        grid=(heads + rounds,),
        in_specs=[outside] * 6,
        out_specs=[outside] * 5,
        out_shape=[full_t] * 4 + [jax.ShapeDtypeStruct((n, share, heads), BF16)],
        scratch_shapes=[
            vmem((5, heads, rows, width), BF16), vmem((rows, heads_all), BF16),
            vmem((4, heads, rows, width), BF16), vmem((rows, heads), F32), vmem((rows, heads), BF16),
        ] + [narrow] * 2 + [square] * 3 + [state_list] * 3 + [totals] * 2 + [state] * 4
        + [dma((rounds, heads))] * 2 + semaphores(5) + semaphores(4),
        compiler_params=pltpu.CompilerParams(
            dimension_semantics=("arbitrary",), vmem_limit_bytes=60 * 1024 * 1024,
            collective_id=0, has_side_effects=True,
        ),
        name="layer",
    )(queries, key_in, values_in, log_decay, d_out, strength)
    return dq, dk, dv, jnp.transpose(ds, (1, 0, 2)).reshape(share, heads_all), dg


def solution(mesh):
    spec = P(("ctx", "head"), None)
    return jax.shard_map(
        per_device, mesh=mesh, in_specs=(spec,) * 6, out_specs=(spec,) * 5, check_vma=False
    )
```

time: 419 us -> 132 us (0.32)
  the two profiles are of different devices: /device:TPU:2 before, /device:TPU:0 now
where the time goes in v4:
time: 132 us; the launch traced here: 131 us
  Pallas kernels  123 us (93%)
  local copies, waits for them, and re-layouts  8.08 us (6%)
    pallas_call x1, Pallas kernels, per_device(): pl.pallas_call(functools.partial(layer_kernel, n, rounds, SPAN), grid=(he...  123 us
    unnamed x11, local copies, waits for them, and re-layouts  6.57 us

profile of v4, /device:TPU:0, one launch (start us, length us, event | category | flops | bytes accessed | tf_op | source)
XLA Modules:
  0.0 131.2 jit_solution(6013436287963300902)
XLA Ops:
  0.6 1.4 %copy.12.b_ref = bf16[64,32]{1,0:T(8,128)(2,1)} copy(bf16[64,32]{0,1:T(8,128)(2,1)} %param.9) | data formatting | bytes 8192 | tf_op args[3]
  2.0 122.5 %layer.1 = (bf16[64,4096]{1,0:T(8,128)(2,1)}, bf16[64,4096]{1,0:T(8,128)(2,1)}, bf16[64,4096]{1,0:T(8,128)(2,1)}, bf16[64,4096]{1,0:T(8,128)(2,1)}, bf16[4,64,8]{2,1,0:T(8,128)(2,1)}) custom-call(bf16[64,4096]{1,0:T(8,128)(2,1)} %q_ref.1, bf16[64,4096]{1,0:T(8,128)(2,1)} %k_ref.1, bf16[64,4096]{1,0:T(8,128)(2,1)} %v_ref.1, bf16[64,4096]{1,0:T(8,128)(2,1)} %g_ref.1, ...), custom_call_target="tpu_custom_call" | custom-call | tf_op jit(solution)/shard_map/layer/pallas_call | solution.py:515
  124.5 1.5 %copy.13 = bf16[64,4,8]{0,2,1:T(8,128)(2,1)} copy(bf16[64,4,8]{2,0,1:T(8,128)(2,1)} %bitcast.2) | data formatting | bytes 8192 | tf_op jit(solution)/shard_map/transpose | solution.py:532
  126.1 0.0 copy-start.2
  126.1 1.9 %copy.18 = bf16[64,4096]{1,0:T(8,128)(2,1)} copy(bf16[64,4096]{1,0:T(8,128)(2,1)} %get-tuple-element.20) | data formatting | bytes 1048576
  128.0 0.0 copy-done.2
  128.0 0.0 copy-start.1
  128.0 0.8 copy.19
  128.8 0.4 copy-done.1
  129.2 0.0 copy-start
  129.2 0.8 copy.20
  130.0 0.4 copy-done
  130.4 0.8 copy.21
Async XLA Ops:
  126.1 1.9 %copy-start.2 = (bf16[64,4096]{1,0:T(8,128)(2,1)S(1)}, bf16[64,4096]{1,0:T(8,128)(2,1)}, u32[]{:S(2)}) copy-start(bf16[64,4096]{1,0:T(8,128)(2,1)} %get-tuple-element.21) | copy-start | bytes 1572868
  128.0 1.2 copy-start.1
  129.2 1.2 copy-start

commit v5 on v4

--- a/solution.py
+++ b/solution.py
@@ -75,8 +75,13 @@
 
 
 def column_of(table, index):
-    lane = lax.broadcasted_iota(jnp.int32, table.shape, 1)
-    return jnp.sum(jnp.where(lane == index, table, 0.0), axis=1, keepdims=True)
+    parts, heads, share = table.shape
+    row, col = grids(share)
+    head = lax.broadcasted_iota(jnp.int32, (heads, share), 0)
+    lines = [jnp.sum(jnp.where(head == index, table[p], 0.0), axis=0, keepdims=True) for p in range(parts)]
+    return jnp.concatenate(
+        [jnp.sum(jnp.where(row == col, line, 0.0), axis=1, keepdims=True) for line in lines], axis=0
+    )
 
 
 def norm_of(x):
@@ -123,11 +128,11 @@
         )
 
     def table_local():
-        return pltpu.make_async_copy(table_ref, table_held.at[mine], t_own)
+        return pltpu.make_async_copy(table_ref, table_held.at[me], t_own)
 
     def table_remote(step):
         return pltpu.make_async_remote_copy(
-            src_ref=table_ref, dst_ref=table_held.at[mine], send_sem=t_send.at[step],
+            src_ref=table_ref, dst_ref=table_held.at[me], send_sem=t_send.at[step],
             recv_sem=t_recv.at[step], device_id={"head": lax.rem(me + step, n)}, device_id_type=MESH,
         )
 
@@ -253,12 +258,12 @@
         )
 
     def table_local():
-        return pltpu.make_async_copy(db_done.at[part(me)], db_out.at[me], t_own)
+        return pltpu.make_async_copy(db_done.at[me], db_out.at[me], t_own)
 
     def table_remote(step):
         peer = lax.rem(me + step, n)
         return pltpu.make_async_remote_copy(
-            src_ref=db_done.at[part(peer)], dst_ref=db_out.at[me], send_sem=t_send.at[step],
+            src_ref=db_done.at[peer], dst_ref=db_out.at[me], send_sem=t_send.at[step],
             recv_sem=t_recv.at[step], device_id={"head": peer}, device_id_type=MESH,
         )
 
@@ -330,8 +335,13 @@
     emit(0, d_value)
     residue = d_update - dot3(split(a_ref[h].T), d_value_s)
     d_beta = jnp.sum(error * residue, axis=1, keepdims=True)
-    lane = lax.broadcasted_iota(jnp.int32, db_all.shape, 1)
-    db_all[...] = jnp.where(lane == h, d_beta, db_all[...])
+    parts, _, share = db_all.shape
+    at_row, at_col = grids(share)
+    sublane = lax.broadcasted_iota(jnp.int32, (heads, share), 0)
+    for p in range(parts):
+        piece = d_beta[p * share : (p + 1) * share]
+        line = jnp.sum(jnp.where(at_row == at_col, piece, 0.0), axis=0, keepdims=True)
+        db_all[p] = jnp.where(sublane == h, line, db_all[p])
     dq_head = each(lambda i, at: dot3(o[at : at + span], states_s[i], NT))
     dk_head = -each(lambda i, at: dot3(rows_of(d_value_s, at, span), states_s[i], NT))
     dk_tail = each(lambda i, at: dot3(rows_of(update_s, at, span), grads_s[i], NT))
@@ -517,10 +527,10 @@
         grid=(heads + rounds,),
         in_specs=[outside] * 6,
         out_specs=[outside] * 5,
-        out_shape=[full_t] * 4 + [jax.ShapeDtypeStruct((n, share, heads), BF16)],
+        out_shape=[full_t] * 4 + [jax.ShapeDtypeStruct((n, heads, share), BF16)],
         scratch_shapes=[
-            vmem((5, heads, rows, width), BF16), vmem((rows, heads_all), BF16),
-            vmem((4, heads, rows, width), BF16), vmem((rows, heads), F32), vmem((rows, heads), BF16),
+            vmem((5, heads, rows, width), BF16), vmem((n, heads_all, share), BF16),
+            vmem((4, heads, rows, width), BF16), vmem((n, heads, share), F32), vmem((n, heads, share), BF16),
         ] + [narrow] * 2 + [square] * 3 + [state_list] * 3 + [totals] * 2 + [state] * 4
         + [dma((rounds, heads))] * 2 + semaphores(5) + semaphores(4),
         compiler_params=pltpu.CompilerParams(
@@ -528,8 +538,8 @@
             collective_id=0, has_side_effects=True,
         ),
         name="layer",
-    )(queries, key_in, values_in, log_decay, d_out, strength)
-    return dq, dk, dv, jnp.transpose(ds, (1, 0, 2)).reshape(share, heads_all), dg
+    )(queries, key_in, values_in, log_decay, d_out, strength.T)
+    return dq, dk, dv, ds.reshape(heads_all, share).T, dg
 
 
 def solution(mesh):

time: 132 us -> 128 us (0.970)
  local copies, waits for them, and re-layouts: 8.08 us -> 5.35 us
    transpose x1 -> x0, local copies, waits for them, and re-layouts: 1.51 us -> none  [per_device(): jnp.transpose(ds, (1, 0, 2)).reshape(share, heads_all)]
    unnamed x11 -> x13, local copies, waits for them, and re-layouts: 6.57 us -> 5.35 us
where the time goes in v5:
time: 128 us
  Pallas kernels  122 us (95%)
  local copies, waits for them, and re-layouts  5.35 us (4%)
    pallas_call x1, Pallas kernels, per_device(): pl.pallas_call(functools.partial(layer_kernel, n, rounds, SPAN), grid=(he...  122 us
    unnamed x13, local copies, waits for them, and re-layouts  5.35 us

profile of v5, /device:TPU:0, one launch (start us, length us, event | category | flops | bytes accessed | tf_op | source)
XLA Modules:
  0.0 127.5 jit_solution(4886750240754041065)
XLA Ops:
  0.6 121.5 %layer.1 = (bf16[64,4096]{1,0:T(8,128)(2,1)}, bf16[64,4096]{1,0:T(8,128)(2,1)}, bf16[64,4096]{1,0:T(8,128)(2,1)}, bf16[64,4096]{1,0:T(8,128)(2,1)}, bf16[4,8,64]{2,1,0:T(8,128)(2,1)}) custom-call(bf16[64,4096]{1,0:T(8,128)(2,1)} %q_ref.1, bf16[64,4096]{1,0:T(8,128)(2,1)} %k_ref.1, bf16[64,4096]{1,0:T(8,128)(2,1)} %v_ref.1, bf16[64,4096]{1,0:T(8,128)(2,1)} %g_ref.1, ...), custom_call_target="tpu_custom_call" | custom-call | tf_op jit(solution)/shard_map/layer/pallas_call | solution.py:525
  122.2 0.0 copy-start.2
  122.2 1.9 %copy.16 = bf16[64,4096]{1,0:T(8,128)(2,1)} copy(bf16[64,4096]{1,0:T(8,128)(2,1)} %get-tuple-element.20) | data formatting | bytes 1048576
  124.1 0.0 copy-done.2
  124.1 0.0 copy-start.1
  124.1 0.8 copy.17
  124.9 0.4 copy-done.1
  125.4 0.0 copy-start.3
  125.4 0.0 copy-start
  125.4 0.8 copy.18
  126.2 0.0 copy-done.3
  126.2 0.6 copy.19
  126.8 0.0 copy-done
  126.8 0.8 copy.20
Async XLA Ops:
  122.2 1.9 %copy-start.2 = (bf16[64,4096]{1,0:T(8,128)(2,1)S(1)}, bf16[64,4096]{1,0:T(8,128)(2,1)}, u32[]{:S(2)}) copy-start(bf16[64,4096]{1,0:T(8,128)(2,1)} %get-tuple-element.21) | copy-start | bytes 1572868
  124.1 1.2 copy-start.1
  125.4 0.8 copy-start.3
  125.4 1.4 %copy-start = (bf16[64,4096]{1,0:T(8,128)(2,1)S(1)}, bf16[64,4096]{1,0:T(8,128)(2,1)}, u32[]{:S(2)}) copy-start(bf16[64,4096]{1,0:T(8,128)(2,1)} %get-tuple-element.24) | copy-start | bytes 1572868
